TPU v7x, 32 devices: a whole 2x2x4 slice. The times are simulated.
32 devices in a mesh: grp: 2 (over y), chan: 4 (over z), sub: 4 (over x, core).
Axes of the slice: x: 2, y: 2, z: 4, core: 2. Of those that a mesh axis runs over, the one named last changes fastest.
Arguments:
- voltages: bfloat16 [2048, 2, 5504], P(('grp', 'chan', 'sub')), parts along dimension 0, may hold values from -6 to 6
- taps: float32 [1536], replicated, may hold values from -0.15625 to 0.15625
- input_id: int32 [1024], replicated, may hold values from 0 to 1023, each once
- counts: int32 [8], P('grp'), parts along dimension 0, may hold values from 2 to 8, as said below
- delays: int32 [512, 1024], P(('grp', 'sub')), parts along dimension 0, may hold values from 0 to 127
- beam_owner: int32 [512, 1], P('grp'), parts along dimension 0, may hold values from 0 to 3; in each aligned block of 64 rows (0 to 63, 64 to 127, ...) at most 32 rows name the same one
Outputs:
- visibility: bfloat16 [256, 2, 1024, 1024], P(('grp', 'chan'), None, 'sub'), parts along dimension 0
- resynth: float32 [1024, 2, 5504], P(('grp', 'chan', 'sub')), parts along dimension 0
There are 2 independent parts, one for each index of `grp`. A program takes and returns all parts, laid end to end along the dimension named above; an argument that names none is the same for every part. Nothing has to cross between parts.
Inputs may be any that keep to these rules, and one draw needn't show every extreme that they name: `input_id`: each input id appears once. `counts`: every draw has a block with all 8 spectra valid. `beam_owner`: within each section of 64 consecutive beams no owner is named more than 32 times; some owner is named exactly 32 times in some section.
All inputs are finite; a program needn't handle non-finite values.
Results may differ from a plain program's by a relative error of at most 0.007.
Values may be sent and summed in bfloat16 or wider, within the bound.
A program may use at most 192 MiB of HBM per device.

v0:
```python
import functools
import math

import jax
import jax.numpy as jnp
from jax import lax
from jax.experimental import pallas as pl
from jax.experimental.pallas import tpu as pltpu
from jax.sharding import PartitionSpec as P

NCH = 128
TAPS = 12
SPEC = 8
BLOCKS = 4
BEAMS = 256


def filter_table(taps, chans):
    length = taps.shape[0]
    position = jnp.arange(length, dtype=jnp.int32) % chans
    channel = jnp.arange(chans, dtype=jnp.int32)
    phase = (position[:, None] * channel[None, :] % chans).astype(jnp.float32) * (
        2.0 * math.pi / chans
    )
    cosine = taps[:, None] * jnp.cos(phase)
    sine = taps[:, None] * jnp.sin(phase)
    upper = jnp.concatenate([cosine, -sine], axis=1)
    lower = jnp.concatenate([sine, cosine], axis=1)
    return jnp.concatenate([upper, lower], axis=0).astype(jnp.bfloat16)


def resynthesize(received, table, taps_count, chans):
    count = received.shape[0]
    spectra_n = received.shape[3]
    table3 = table.reshape(2 * taps_count * chans, 2, chans)
    grid = jnp.einsum("pcht,mch->ptm", received, table3, preferred_element_type=jnp.float32)
    grid = grid.reshape(count, spectra_n, 2, taps_count, chans)
    total = jnp.zeros((count, spectra_n + taps_count - 1, 2, chans), jnp.float32)
    for k in range(taps_count):
        total = total + jnp.pad(
            grid[:, :, :, k, :], ((0, 0), (k, taps_count - 1 - k), (0, 0), (0, 0))
        )
    return jnp.transpose(total, (0, 2, 1, 3)).reshape(
        count, 2, (spectra_n + taps_count - 1) * chans
    )


def local_plain(voltages, taps, input_id, counts, delays, beam_owner):
    n_chan = lax.axis_size("chan")
    n_sub = lax.axis_size("sub")
    inp_dev = voltages.shape[0]
    inputs = input_id.shape[0]
    chans = NCH
    taps_count = TAPS
    spectra_n = BLOCKS * SPEC
    ch_dev = chans // n_chan
    rows = inputs // n_sub
    section = BEAMS // n_sub
    most = min(section, max(2, 2 * section // n_chan))
    table = filter_table(taps, chans)
    position = jnp.arange(spectra_n, dtype=jnp.int32)
    valid = (position % SPEC < jnp.repeat(counts, SPEC)).astype(jnp.float32)
    total = jnp.sum(counts.astype(jnp.float32))
    frames = voltages.reshape(inp_dev, 2, spectra_n + taps_count - 1, chans)
    windows = jnp.concatenate(
        [frames[:, :, k : k + spectra_n, :] for k in range(taps_count)], axis=3
    )
    table3 = table.reshape(2, taps_count * chans, 2 * chans)
    filtered = jnp.einsum("icth,chm->mit", windows, table3, preferred_element_type=jnp.float32)
    filtered = filtered * valid[None, None, :]
    spectra = filtered.reshape(2, chans, inp_dev, spectra_n).astype(jnp.bfloat16)
    slot_of = jnp.zeros((inputs,), jnp.int32).at[input_id].set(jnp.arange(inputs, dtype=jnp.int32))
    turned = lax.all_to_all(spectra, "chan", split_axis=1, concat_axis=2, tiled=True)
    gathered = lax.all_gather(turned, "sub", axis=2, tiled=True)
    chan_part = slot_of // (n_sub * inp_dev)
    sub_part = slot_of // inp_dev % n_sub
    order = (sub_part * n_chan + chan_part) * inp_dev + slot_of % inp_dev
    by_id = jnp.take(gathered, order, axis=2)
    sub_index = lax.axis_index("sub")
    mine = lax.dynamic_slice_in_dim(by_id, sub_index * rows, rows, 2)
    real_part = jnp.einsum("cxit,cxjt->xij", mine, by_id, preferred_element_type=jnp.float32)
    imag_part = jnp.einsum("xit,xjt->xij", mine[1], by_id[0], preferred_element_type=jnp.float32)
    imag_part = imag_part - jnp.einsum(
        "xit,xjt->xij", mine[0], by_id[1], preferred_element_type=jnp.float32
    )
    visibility = (jnp.stack([real_part, imag_part], axis=1) / total).astype(jnp.bfloat16)
    channel = lax.axis_index("chan") * ch_dev + jnp.arange(ch_dev, dtype=jnp.int32)
    phase = (delays[None, :, :] * channel[:, None, None] % chans).astype(jnp.float32) * (
        2.0 * math.pi / chans
    )
    scale = 1.0 / math.sqrt(inputs)
    weight_cos = (jnp.cos(phase) * scale).astype(jnp.bfloat16)
    weight_sin = (jnp.sin(phase) * scale).astype(jnp.bfloat16)
    from_cos = jnp.einsum("xbi,cxit->cxbt", weight_cos, by_id, preferred_element_type=jnp.float32)
    from_sin = jnp.einsum("xbi,cxit->cxbt", weight_sin, by_id, preferred_element_type=jnp.float32)
    beams = jnp.stack([from_cos[0] - from_sin[1], from_cos[1] + from_sin[0]]).astype(jnp.bfloat16)
    owner = lax.dynamic_slice_in_dim(beam_owner[:, 0], sub_index * section, section)
    beam = jnp.arange(section, dtype=jnp.int32)
    earlier = (owner[None, :] == owner[:, None]) & (beam[None, :] < beam[:, None])
    rank = jnp.sum(earlier.astype(jnp.int32), axis=1)
    target = owner * most + rank
    select = (jnp.arange(n_chan * most, dtype=jnp.int32)[:, None] == target[None, :]).astype(
        jnp.bfloat16
    )
    placed = jnp.einsum("pb,cxbt->pcxt", select, beams, preferred_element_type=jnp.float32).astype(
        jnp.bfloat16
    )
    placed = placed.reshape(n_chan, most, 2, ch_dev, spectra_n)
    resynth = resynthesize(
        lax.all_to_all(placed, "chan", split_axis=0, concat_axis=3, tiled=True)[0],
        table,
        taps_count,
        chans,
    )
    return (visibility, resynth)


def filter_kernel(rows, pairs, steps, wide, n_chan, fr_ref, w_ref, mask_ref, out_ref):
    group = 4 if pairs % 4 == 0 else 1
    width = wide // n_chan
    for first in range(0, pairs, group):
        acc = jnp.zeros((group * rows, wide), jnp.float32)
        for k in range(steps):
            window = jnp.concatenate(
                [
                    jnp.concatenate([fr_ref[0, at], fr_ref[1, at]], axis=1)
                    for at in range(2 * first + k, 2 * (first + group) + k, 2)
                ],
                axis=0,
            )
            acc = acc + jnp.dot(window, w_ref[k], preferred_element_type=jnp.float32)
        for j in range(group):
            pair = first + j
            part = (acc[j * rows : (j + 1) * rows] * mask_ref[pair : pair + 1, :]).astype(
                jnp.bfloat16
            )
            for d in range(n_chan):
                out_ref[d, :, pair * width : (pair + 1) * width] = part[
                    :, d * width : (d + 1) * width
                ]


def channelize(voltages, taps, valid, n_chan):
    rows = voltages.shape[0]
    spectra_n = valid.shape[0]
    pairs = spectra_n // 2
    chans, ch_dev = NCH, NCH // n_chan
    steps = TAPS + 1
    frames_n = spectra_n + TAPS - 1
    frames = voltages.reshape(rows, 2, frames_n, chans)
    frames = jnp.transpose(frames, (1, 2, 0, 3))
    wide = 4 * chans
    column = jnp.arange(wide, dtype=jnp.int32)
    dest, rest = column // (4 * ch_dev), column % (4 * ch_dev)
    parity, part, inner = rest // (2 * ch_dev), rest // ch_dev % 2, rest % ch_dev
    channel = dest * ch_dev + inner
    row = jnp.arange(2 * chans, dtype=jnp.int32)
    phase = (row[:, None] % chans * channel[None, :] % chans).astype(jnp.float32) * (
        2.0 * math.pi / chans
    )
    cosine, sine = jnp.cos(phase), jnp.sin(phase)
    lower = row[:, None] >= chans
    trig = jnp.where(
        lower == (part[None, :] == 1), cosine, jnp.where(lower, sine, -sine)
    )
    trig = lax.optimization_barrier(trig)
    taps2 = taps.reshape(TAPS, chans)
    taps2 = jnp.concatenate([taps2, taps2], axis=1)
    even = jnp.pad(taps2, ((0, 1), (0, 0)))
    odd = jnp.pad(taps2, ((1, 0), (0, 0)))
    factor = jnp.where(parity[None, None, :] == 0, even[:, :, None], odd[:, :, None])
    weights = (trig[None] * factor).astype(jnp.bfloat16)
    mask = jnp.where(parity[None, :] == 0, valid[0::2, None], valid[1::2, None])
    return pl.pallas_call(
        functools.partial(filter_kernel, rows, pairs, steps, wide, n_chan),
        out_shape=jax.ShapeDtypeStruct((n_chan, rows, spectra_n * 2 * ch_dev), jnp.bfloat16),
        name="filterbank",
    )(frames, weights, mask)


def turn_of(steps):
    quarter = NCH // 4
    turn = steps & (NCH - 1)
    quadrant = (turn + quarter // 2) >> (quarter.bit_length() - 1)
    x = (turn - quadrant * quarter).astype(jnp.float32) * (2.0 * math.pi / NCH)
    y = x * x
    even = 1.0 + y * (-1 / 2 + y * (1 / 24 + y * (-1 / 720 + y * (1 / 40320))))
    odd = x * (1.0 + y * (-1 / 6 + y * (1 / 120 + y * (-1 / 5040 + y * (1 / 362880)))))
    swap = (quadrant & 1) == 1
    cosine, sine = jnp.where(swap, odd, even), jnp.where(swap, even, odd)
    cosine = jnp.where(((quadrant + 1) & 2) == 2, -cosine, cosine)
    return cosine, jnp.where((quadrant & 2) == 2, -sine, sine)


def weigh(first, scale, delay_ref, out_ref, at, left, high, wide):
    beams_n = delay_ref.shape[0]
    delay = delay_ref[at : at + high, left : left + wide]
    step_cos, step_sin = turn_of(delay)
    cosine, sine = turn_of(delay * first)

    def body(f, held):
        cosine, sine = held
        out_ref[f, at : at + high, left : left + wide] = cosine.astype(jnp.bfloat16)
        low = at + beams_n
        out_ref[f, low : low + high, left : left + wide] = sine.astype(jnp.bfloat16)
        return (
            cosine * step_cos - sine * step_sin,
            sine * step_cos + cosine * step_sin,
        )

    lax.fori_loop(0, out_ref.shape[0], body, (cosine * scale, sine * scale))


def turn_kernel(n_chan, n_sub, pieces, scale, x_ref, delay_ref, g_ref, weight_ref, own_sem, zs, zr, xs, xr, cs, cr):
    me_c, me_s = lax.axis_index("chan"), lax.axis_index("sub")
    core, across = me_s % 2, me_s // 2
    n_x = n_sub // 2
    twin = me_s + 1 - 2 * core
    rows = x_ref.shape[1] // pieces
    mesh_id = pl.DeviceIdType.MESH

    def chan_of(offset):
        return (me_c + offset) % n_chan

    def sub_of(offset):
        return (across + offset) % n_x * 2 + core

    barrier = pltpu.get_barrier_semaphore()
    for j in range(1, n_chan):
        pl.semaphore_signal(barrier, device_id={"chan": chan_of(j)}, device_id_type=mesh_id)
    for j in range(1, n_x):
        pl.semaphore_signal(barrier, device_id={"sub": sub_of(j)}, device_id_type=mesh_id)
    pl.semaphore_signal(barrier, device_id={"sub": twin}, device_id_type=mesh_id)
    pl.semaphore_wait(barrier, n_chan + n_x - 1)

    def place(ref, piece):
        return ref.at[piece * rows : (piece + 1) * rows]

    def z_copy(j, h):
        return pltpu.make_async_remote_copy(
            src_ref=place(x_ref.at[chan_of(j)], h),
            dst_ref=place(g_ref.at[me_s, me_c], h),
            send_sem=zs.at[j, h],
            recv_sem=zr.at[j, h],
            device_id={"chan": chan_of(j)},
            device_id_type=mesh_id,
        )

    def source(sub, j, h):
        if j == 0:
            return place(x_ref.at[me_c], h)
        return place(g_ref.at[sub, chan_of(n_chan - j)], h)

    def x_copy(dx, j, h):
        return pltpu.make_async_remote_copy(
            src_ref=source(me_s, j, h),
            dst_ref=place(g_ref.at[me_s, chan_of(n_chan - j)], h),
            send_sem=xs.at[dx, j, h],
            recv_sem=xr.at[dx, j, h],
            device_id={"sub": sub_of(dx)},
            device_id_type=mesh_id,
        )

    def core_copy(dx, j, h):
        home = sub_of(n_x - dx)
        block = place(g_ref.at[home, chan_of(n_chan - j)], h)
        return pltpu.make_async_remote_copy(
            src_ref=source(me_s, j, h) if dx == 0 else block,
            dst_ref=block,
            send_sem=cs.at[dx, j, h],
            recv_sem=cr.at[dx, j, h],
            device_id={"sub": twin},
            device_id_type=mesh_id,
        )

    own = pltpu.make_async_copy(x_ref.at[me_c], g_ref.at[me_s, me_c], own_sem)
    started = []
    for h in range(pieces):
        for j in range(1, n_chan):
            copy = z_copy(j, h)
            copy.start()
            started.append(copy)
    own.start()

    def spread(j, h):
        for dx in range(1, n_x):
            copy = x_copy(dx, j, h)
            copy.start()
            started.append(copy)
        copy = core_copy(0, j, h)
        copy.start()
        started.append(copy)

    for h in range(pieces):
        spread(0, h)
    ch_dev = weight_ref.shape[0]
    beams_n, inputs = delay_ref.shape
    high, wide = 16, 512
    units = [(at, left) for at in range(0, beams_n, high) for left in range(0, inputs, wide)]

    def work():
        if units:
            at, left = units.pop(0)
            weigh(me_c * ch_dev, scale, delay_ref, weight_ref, at, left, high, wide)

    def relay(h):
        for j in range(n_chan):
            work()
            for dx in range(1, n_x):
                x_copy(dx, j, h).wait_recv()
                copy = core_copy(dx, j, h)
                copy.start()
                started.append(copy)

    for h in range(pieces):
        for j in range(1, n_chan):
            work()
            z_copy(j, h).wait_recv()
            spread(j, h)
        if h > 0:
            relay(h - 1)
    relay(pieces - 1)
    while units:
        work()
    for h in range(pieces):
        for j in range(n_chan):
            for dx in range(n_x):
                core_copy(dx, j, h).wait_recv()
    for copy in started:
        copy.wait_send()
    own.wait()


def corner_turn(blocks, delays, n_chan, n_sub):
    pieces = 2
    dma = pltpu.SemaphoreType.DMA
    n_x = n_sub // 2
    beams_n, inputs = delays.shape
    return pl.pallas_call(
        functools.partial(turn_kernel, n_chan, n_sub, pieces, 1.0 / math.sqrt(inputs)),
        out_shape=[
            jax.ShapeDtypeStruct((n_sub,) + blocks.shape, jnp.bfloat16),
            jax.ShapeDtypeStruct((NCH // n_chan, 2 * beams_n, inputs), jnp.bfloat16),
        ],
        in_specs=[pl.BlockSpec(memory_space=pltpu.VMEM)] * 2,
        out_specs=[pl.BlockSpec(memory_space=pl.ANY), pl.BlockSpec(memory_space=pltpu.VMEM)],
        scratch_shapes=[
            dma,
            dma((n_chan, pieces)),
            dma((n_chan, pieces)),
            dma((n_x, n_chan, pieces)),
            dma((n_x, n_chan, pieces)),
            dma((n_x, n_chan, pieces)),
            dma((n_x, n_chan, pieces)),
        ],
        compiler_params=pltpu.CompilerParams(collective_id=0, has_side_effects=True),
        name="corner_turn",
    )(blocks, delays)


def beam_kernel(ch_dev, spectra_n, n_chan, batch, g_ref, perm_ref, weight_ref, sel_ref, id_ref, out_ref, held, ready, own_sem, send, recv):
    step = pl.program_id(0)
    pair = weight_ref.shape[0]
    steps = ch_dev // pair
    me_c = lax.axis_index("chan")
    mesh_id = pl.DeviceIdType.MESH

    @pl.when(step == 0)
    def _():
        barrier = pltpu.get_barrier_semaphore()
        for j in range(1, n_chan):
            pl.semaphore_signal(
                barrier, device_id={"chan": (me_c + j) % n_chan}, device_id_type=mesh_id
            )
        wide = min(256, g_ref.shape[1])

        @pl.loop(0, g_ref.shape[1] // wide)
        def _(m):
            at = pl.multiple_of(m * wide, wide)
            sorted_part = lax.dot_general(
                g_ref[:, pl.ds(at, wide)],
                perm_ref[...],
                (((0,), (0,)), ((), ())),
                preferred_element_type=jnp.float32,
            )
            per = 2 * ch_dev
            for q in range(wide // per):
                to = pl.multiple_of((m * (wide // per) + q) * (per + 8), 8)
                for tile in range(held.shape[0]):
                    held[tile, pl.ds(to, per), :] = sorted_part[
                        q * per : (q + 1) * per, tile * 128 : (tile + 1) * 128
                    ]

        pl.semaphore_wait(barrier, n_chan - 1)

    def rows_of(start):
        every = pl.ds(start, spectra_n, stride=2 * ch_dev + 8)
        return jnp.concatenate([held[tile, every, :] for tile in range(held.shape[0])], axis=1)

    def form(j):
        f = step * pair + j
        both = jnp.concatenate([rows_of(f), rows_of(f + ch_dev)], axis=0).astype(jnp.bfloat16)
        id_ref[j] = both
        mixed = lax.dot_general(
            weight_ref[j], both, (((1,), (1,)), ((), ())), preferred_element_type=jnp.float32
        )
        beams_n = mixed.shape[0] // 2
        upper, lower = mixed[:beams_n], mixed[beams_n:]
        beam_re = upper[:, :spectra_n] - lower[:, spectra_n:]
        beam_im = upper[:, spectra_n:] + lower[:, :spectra_n]
        return [beam_re, beam_im]

    beams = jnp.concatenate(form(0) + form(1), axis=1).astype(jnp.bfloat16)
    placed = jnp.dot(sel_ref[...], beams, preferred_element_type=jnp.float32).astype(jnp.bfloat16)
    most = placed.shape[0] // n_chan
    for d in range(n_chan):
        ready[d, step] = placed[d * most : (d + 1) * most]

    def copy_of(b, j):
        to = (me_c + j) % n_chan
        return pltpu.make_async_remote_copy(
            src_ref=ready.at[to, pl.ds(b * batch, batch)],
            dst_ref=out_ref.at[me_c, pl.ds(b * batch, batch)],
            send_sem=send.at[b, j],
            recv_sem=recv.at[b, j],
            device_id={"chan": to},
            device_id_type=mesh_id,
        )

    for b in range(steps // batch):

        @pl.when(step == (b + 1) * batch - 1)
        def _():
            for j in range(1, n_chan):
                copy_of(b, j).start()

    @pl.when(step == steps - 1)
    def _():
        own = pltpu.make_async_copy(ready.at[me_c], out_ref.at[me_c], own_sem)
        own.start()
        for b in range(steps // batch):
            for j in range(1, n_chan):
                copy_of(b, j).wait_recv()
        for b in range(steps // batch):
            for j in range(1, n_chan):
                copy_of(b, j).wait_send()
        own.wait()


def form_beams(gathered, perm, weights, select, spectra_n, n_chan):
    inputs = perm.shape[0]
    ch_dev, double_n, _ = weights.shape
    slots, beams_n = select.shape
    cols = gathered.shape[1]
    pair = 2
    steps = ch_dev // pair
    batch = steps // 4
    dma = pltpu.SemaphoreType.DMA
    whole = lambda shape: pl.BlockSpec(
        shape, lambda f: (0,) * len(shape), pipeline_mode=pl.Buffered(1)
    )
    travel = (n_chan, steps, slots // n_chan, 2 * pair * spectra_n)
    return pl.pallas_call(
        functools.partial(beam_kernel, ch_dev, spectra_n, n_chan, batch),
        grid=(steps,),
        in_specs=[
            whole((inputs, cols)),
            whole((inputs, inputs)),
            pl.BlockSpec((pair, double_n, inputs), lambda f: (f, 0, 0)),
            whole((slots, beams_n)),
        ],
        out_specs=[
            pl.BlockSpec((pair, 2 * spectra_n, inputs), lambda f: (f, 0, 0)),
            pl.BlockSpec(memory_space=pl.ANY),
        ],
        scratch_shapes=[
            pltpu.VMEM((inputs // 128, cols + 8 * spectra_n, 128), jnp.float32),
            pltpu.VMEM(travel, jnp.bfloat16),
            dma,
            dma((4, n_chan)),
            dma((4, n_chan)),
        ],
        out_shape=[
            jax.ShapeDtypeStruct((ch_dev, 2 * spectra_n, inputs), jnp.bfloat16),
            jax.ShapeDtypeStruct(travel, jnp.bfloat16),
        ],
        compiler_params=pltpu.CompilerParams(
            dimension_semantics=("arbitrary",), collective_id=1, has_side_effects=True
        ),
        name="beams",
    )(gathered, perm, weights, select)


def visibility_kernel(sub_ref, scale_ref, left_ref, right_ref, out_ref):
    for j in range(left_ref.shape[0]):
        left = left_ref[j]
        half, rows = left.shape[0] // 2, left.shape[1]
        turned = jnp.concatenate([left[half:], -left[:half]], axis=0)
        both = jnp.concatenate([left, turned], axis=1)
        product = lax.dot_general(
            both, right_ref[j], (((0,), (0,)), ((), ())), preferred_element_type=jnp.float32
        )
        product = (product * scale_ref[0]).astype(jnp.bfloat16)
        out_ref[j, 0] = product[:rows]
        out_ref[j, 1] = product[rows:]


def correlate(by_id, scale, sub_index, rows):
    ch_dev, depth, inputs = by_id.shape
    group = 2 if ch_dev % 2 == 0 else 1
    return pl.pallas_call(
        visibility_kernel,
        grid_spec=pltpu.PrefetchScalarGridSpec(
            num_scalar_prefetch=1,
            grid=(ch_dev // group,),
            in_specs=[
                pl.BlockSpec(memory_space=pltpu.SMEM),
                pl.BlockSpec((group, depth, rows), lambda f, s: (f, 0, s[0])),
                pl.BlockSpec((group, depth, inputs), lambda f, s: (f, 0, 0)),
            ],
            out_specs=pl.BlockSpec((group, 2, rows, inputs), lambda f, s: (f, 0, 0, 0)),
        ),
        out_shape=jax.ShapeDtypeStruct((ch_dev, 2, rows, inputs), jnp.bfloat16),
        cost_estimate=pl.CostEstimate(
            flops=4 * ch_dev * rows * inputs * depth,
            bytes_accessed=4 * ch_dev * rows * inputs,
            transcendentals=0,
        ),
        name="visibility",
    )(sub_index, scale, by_id, by_id)


def voice_kernel(spectra_n, count, frames_n, b_ref, w_ref, out_ref):
    chans = w_ref.shape[2] // 2
    group = 4
    for first in range(0, frames_n, group):
        size = min(group, frames_n - first)
        acc = jnp.zeros((size * count, w_ref.shape[2]), jnp.float32)
        for k in range(TAPS):
            low = first - k
            if low + size <= 0 or low >= spectra_n:
                continue
            start = (low + TAPS - 1) * count
            acc = acc + jnp.dot(
                b_ref[start : start + size * count, :], w_ref[k], preferred_element_type=jnp.float32
            )
        for j in range(size):
            at = (first + j) * chans
            for c in range(2):
                out_ref[:, c, at : at + chans] = acc[
                    j * count : (j + 1) * count, c * chans : (c + 1) * chans
                ]


def synthesize(received, taps):
    n_chan, steps, count, width = received.shape
    spectra_n = BLOCKS * SPEC
    pair = width // (2 * spectra_n)
    chans = n_chan * steps * pair
    frames_n = spectra_n + TAPS - 1
    bank = received.reshape(n_chan * steps, count, pair, 2, spectra_n)
    bank = jnp.transpose(bank, (4, 1, 3, 0, 2)).reshape(spectra_n, count, 2 * chans)
    bank = jnp.pad(bank, ((TAPS - 1, TAPS - 1), (0, 0), (0, 0))).reshape(-1, 2 * chans)
    index = jnp.arange(2 * chans, dtype=jnp.int32)
    inner = index % chans
    phase = (inner[:, None] * inner[None, :] % chans).astype(jnp.float32) * (2.0 * math.pi / chans)
    cosine, sine = jnp.cos(phase), jnp.sin(phase)
    from_im, to_im = index[:, None] >= chans, index[None, :] >= chans
    trig = jnp.where(from_im == to_im, cosine, jnp.where(to_im, sine, -sine))
    trig = lax.optimization_barrier(trig)
    taps2 = taps.reshape(TAPS, 1, chans)
    weights = (trig[None] * jnp.concatenate([taps2, taps2], axis=2)).astype(jnp.bfloat16)
    return pl.pallas_call(
        functools.partial(voice_kernel, spectra_n, count, frames_n),
        out_shape=jax.ShapeDtypeStruct((count, 2, frames_n * chans), jnp.float32),
        name="voices",
    )(bank, weights)


def local(voltages, taps, input_id, counts, delays, beam_owner):
    n_chan = lax.axis_size("chan")
    n_sub = lax.axis_size("sub")
    inp_dev = voltages.shape[0]
    inputs = input_id.shape[0]
    chans = NCH
    spectra_n = BLOCKS * SPEC
    ch_dev = chans // n_chan
    rows = inputs // n_sub
    section = BEAMS // n_sub
    most = min(section, max(2, 2 * section // n_chan))
    if inp_dev % 32 or 4 * ch_dev % 128 or rows % 128 or n_sub % 2 or most % 16:
        return local_plain(voltages, taps, input_id, counts, delays, beam_owner)
    position = jnp.arange(spectra_n, dtype=jnp.int32)
    valid = (position % SPEC < jnp.repeat(counts, SPEC)).astype(jnp.float32)
    total = jnp.sum(counts.astype(jnp.float32))
    sub_index = lax.axis_index("sub")
    blocks = channelize(voltages, taps, valid, n_chan)
    gathered, weights = corner_turn(blocks, delays, n_chan, n_sub)
    gathered = gathered.reshape(inputs, -1)
    names = jnp.transpose(input_id.reshape(n_chan, n_sub, inp_dev), (1, 0, 2)).reshape(inputs)
    perm = (names[:, None] == jnp.arange(inputs, dtype=jnp.int32)[None, :]).astype(jnp.bfloat16)
    owner = lax.dynamic_slice_in_dim(beam_owner[:, 0], sub_index * section, section)
    beam = jnp.arange(section, dtype=jnp.int32)
    earlier = (owner[None, :] == owner[:, None]) & (beam[None, :] < beam[:, None])
    rank = jnp.sum(earlier.astype(jnp.int32), axis=1)
    target = owner * most + rank
    select = (jnp.arange(n_chan * most, dtype=jnp.int32)[:, None] == target[None, :]).astype(
        jnp.bfloat16
    )
    by_id, received = form_beams(gathered, perm, weights, select, spectra_n, n_chan)
    visibility = correlate(by_id, (1.0 / total)[None], sub_index.astype(jnp.int32)[None], rows)
    resynth = synthesize(received, taps)
    return (visibility, resynth)


def solution(mesh):
    placed = (
        P(("grp", "chan", "sub"), None, None),
        P(),
        P(),
        P("grp"),
        P(("grp", "sub"), None),
        P("grp", None),
    )
    return jax.shard_map(
        local,
        mesh=mesh,
        in_specs=placed,
        out_specs=(P(("grp", "chan"), None, "sub", None), P(("grp", "chan", "sub"), None, None)),
        check_vma=False,
    )
```

profile of v0, /device:TPU:0, one launch (start us, length us, event | category | flops | bytes accessed | tf_op | source)
XLA Modules:
  0.0 131.7 jit_solution(11816907523933087985)
XLA Ops:
  0.6 0.0 copy-start.1
  0.6 1.3 convert_reduce_fusion.1
  2.6 3.7 %reshape.198 = bf16[64,2,43,128]{3,2,1,0:T(8,128)(2,1)S(1)} reshape(bf16[64,2,5504]{2,1,0:T(2,128)(2,1)} %param.6) | data formatting | bytes 2818048 | tf_op jit(solution)/shard_map/reshape | solution.py:150
  6.3 0.0 copy-start.3
  6.3 1.6 %copy.27 = bf16[64,2,43,128]{3,0,2,1:T(8,128)(2,1)} copy(bf16[64,2,43,128]{3,2,1,0:T(8,128)(2,1)S(1)} %reshape.198) | data formatting | bytes 2818048 | tf_op jit(solution)/shard_map/reshape | solution.py:150
  7.9 0.0 copy-done.1
  8.0 2.2 %fusion.3 = f32[256,512]{1,0:T(8,128)S(1)} fusion(s32[512]{0:T(512)S(1)} %fusion.15, s32[256]{0:T(256)S(1)} %and_select_fusion.1, pred[512]{0:T(512)(128)(4,1)S(1)} %fusion.12, pred[256]{0:T(512)(128)(4,1)S(1)} %iota_compare_fusion.3), kind=kLoop, calls=%fused_computation.13 | loop fusion | flops 2359296 | bytes 528128 | tf_op jit(solution)/shard_map/jit(_where)/select_n | solution.py:163
  10.2 2.3 %multiply_convert_fusion.w_ref = bf16[13,256,512]{2,1,0:T(8,128)(2,1)} fusion(f32[13,256]{1,0:T(8,128)S(1)} %get-tuple-element.11, f32[13,256]{1,0:T(8,128)S(1)} %get-tuple-element.10, f32[256,512]{1,0:T(8,128)S(1)} %fusion.3, pred[512]{0:T(512)(128)(4,1)S(1)} %fusion.17), kind=kLoop, calls=%fused_computation | loop fusion | flops 5111808 | bytes 3959296 | tf_op jit(solution)/shard_map/convert_element_type | solution.py:172
  12.5 0.0 copy-done.3
  12.5 0.1 broadcast_in_dim.69
  12.6 0.1 reshape.191
  12.7 0.1 slice.7
  12.8 0.1 slice.6
  12.9 0.7 broadcast_select_fusion.mask_ref
  13.6 0.0 copy-start.2
  13.6 7.2 %filterbank.1.x_ref = bf16[4,64,2048]{2,1,0:T(8,128)(2,1)} custom-call(bf16[2,43,64,128]{3,2,1,0:T(8,128)(2,1)} %bitcast.22, bf16[13,256,512]{2,1,0:T(8,128)(2,1)} %multiply_convert_fusion.w_ref, f32[16,512]{1,0:T(8,128)} %broadcast_select_fusion.mask_ref), custom_call_target="tpu_custom_call" | custom-call | tf_op jit(solution)/shard_map/filterbank/pallas_call | solution.py:174
  20.8 0.0 copy-start.4
  20.8 40.3 %corner_turn.1 = (bf16[4,4,64,2048]{3,2,1,0:T(8,128)(2,1)}, bf16[32,128,1024]{2,1,0:T(8,128)(2,1)}) custom-call(bf16[4,64,2048]{2,1,0:T(8,128)(2,1)} %filterbank.1.x_ref, s32[64,1024]{1,0:T(8,128)} %delay_ref.1), custom_call_target="tpu_custom_call" | custom-call | tf_op jit(solution)/shard_map/corner_turn/pallas_call | solution.py:339
  61.1 0.0 copy-done.2
  61.1 0.1 reshape.193
  61.2 0.1 eq.113
  61.3 1.7 %fusion.perm_ref = bf16[1024,1024]{1,0:T(8,128)(2,1)} fusion(s32[1024]{0:T(1024)S(1)} %eq.113), kind=kLoop, calls=%fused_computation.2 | loop fusion | flops 2097152 | bytes 2101248 | tf_op jit(solution)/shard_map/convert_element_type | solution.py:601
  63.0 0.0 copy-done.4
  63.0 0.1 dynamic-slice_bitcast_fusion
  63.1 0.2 convert_reduce_fusion
  63.3 0.1 multiply_add_fusion
  63.4 0.6 fusion.9.sel_ref
  64.0 31.8 %beams.1 = (bf16[32,64,1024]{2,1,0:T(8,128)(2,1)}, bf16[4,16,32,128]{3,2,1,0:T(8,128)(2,1)}) custom-call(bf16[1024,2048]{1,0:T(8,128)(2,1)} %bitcast.23, bf16[1024,1024]{1,0:T(8,128)(2,1)} %fusion.perm_ref, bf16[32,128,1024]{2,1,0:T(8,128)(2,1)} %get-tuple-element.7.weight_ref, bf16[128,64]{1,0:T(8,128)(2,1)} %fusion.9.sel_ref), custom_call_target="tpu_custom_call" | custom-call | tf_op jit(solution)/shard_map/beams/pallas_call | solution.py:463
  95.8 0.0 copy-start
  95.8 19.5 %visibility.1 = bf16[32,2,256,1024]{3,2,1,0:T(8,128)(2,1)} custom-call(s32[1]{0:T(128)} %bitcast.sub_ref, f32[1]{0:T(128)} %bitcast.1.scale_ref, bf16[32,64,1024]{2,1,0:T(8,128)(2,1)} %get-tuple-element.8.left_ref.right_ref, bf16[32,64,1024]{2,1,0:T(8,128)(2,1)} %get-tuple-element.8.left_ref.right_ref), custom_call_target="tpu_custom_call" | custom-call | flops 2147483648 | bytes 33554432 | tf_op jit(solution)/shard_map/visibility/pallas_call | solution.py:511
  115.3 0.0 copy-done
  115.3 0.8 reshape.194
  116.2 3.8 %copy.21 = bf16[32,32,2,64,2]{1,0,4,3,2:T(8,128)(2,1)} copy(bf16[32,32,2,64,2]{0,2,4,1,3:T(2,128)(2,1)S(1)} %bitcast.20) | data formatting | bytes 1048576 | tf_op jit(solution)/shard_map/transpose | solution.py:562
  119.9 2.8 %copy.25 = bf16[32,32,256]{2,1,0:T(8,128)(2,1)S(1)} copy(bf16[32,32,256]{1,0,2:T(8,128)(2,1)} %bitcast.21) | data formatting | bytes 1048576
  122.7 1.0 pad.14.clone
  123.7 1.1 fusion.7
  124.9 1.6 %multiply_convert_fusion.1.w_ref = bf16[12,256,256]{2,1,0:T(8,128)(2,1)} fusion(f32[12,256]{1,0:T(8,128)S(1)} %maximum_bitcast_fusion, f32[256,256]{1,0:T(8,128)S(1)} %fusion.7), kind=kLoop, calls=%fused_computation.3 | loop fusion | flops 1572864 | bytes 1847296 | tf_op jit(solution)/shard_map/convert_element_type | solution.py:572
  126.5 5.3 %voices.1 = f32[32,2,5504]{2,1,0:T(2,128)} custom-call(bf16[1728,256]{1,0:T(8,128)(2,1)} %bitcast.24, bf16[12,256,256]{2,1,0:T(8,128)(2,1)} %multiply_convert_fusion.1.w_ref), custom_call_target="tpu_custom_call" | custom-call | tf_op jit(solution)/shard_map/voices/pallas_call | solution.py:573
  (10 shorter events, 0.1 us)
Async XLA Ops:
  0.6 7.3 %copy-start.1 = (f32[1536]{0:T(1024)S(1)}, f32[1536]{0:T(1024)}, u32[]{:S(2)}) copy-start(f32[1536]{0:T(1024)} %param.7) | copy-start | bytes 18436
  6.3 6.2 %copy-start.3 = (s32[4]{0:T(128)S(1)}, s32[4]{0:T(128)}, u32[]{:S(2)}) copy-start(s32[4]{0:T(128)} %param.9) | copy-start | bytes 52
  13.6 47.5 %copy-start.2 = (s32[1024]{0:T(1024)S(1)}, s32[1024]{0:T(1024)}, u32[]{:S(2)}) copy-start(s32[1024]{0:T(1024)} %param.8) | copy-start | bytes 12292
  20.8 42.3 %copy-start.4 = (s32[256,1]{0,1:T(1,128)S(1)}, s32[256,1]{0,1:T(1,128)}, u32[]{:S(2)}) copy-start(s32[256,1]{0,1:T(1,128)} %param.11) | copy-start | bytes 3076
  95.8 19.5 %copy-start = (bf16[4,16,32,128]{3,2,1,0:T(8,128)(2,1)S(1)}, bf16[4,16,32,128]{3,2,1,0:T(8,128)(2,1)}, u32[]{:S(2)}) copy-start(bf16[4,16,32,128]{3,2,1,0:T(8,128)(2,1)} %get-tuple-element.9) | copy-start | bytes 1572868
where the time goes:
time: 133 us; the launch traced here: 132 us
  Pallas kernels  104 us (78%)
  local copies, waits for them, and re-layouts  14.3 us (11%)
  other arithmetic  11.9 us (9%)
  between operations  1.45 us (1%)
    pallas_call x1, Pallas kernels, corner_turn(): pl.pallas_call(functools.partial(turn_kernel, n_chan, n_sub, pieces, 1.0...  40.3 us
    pallas_call x1, Pallas kernels, form_beams(): pl.pallas_call(functools.partial(beam_kernel, ch_dev, spectra_n, n_chan,...  31.8 us
    pallas_call x1, Pallas kernels, correlate(): pl.pallas_call(visibility_kernel, grid_spec=pltpu.PrefetchScalarGridSpec(...  19.5 us
    pallas_call x1, Pallas kernels, channelize(): pl.pallas_call(functools.partial(filter_kernel, rows, pairs, steps, wide,...  7.18 us
    reshape x2, local copies, waits for them, and re-layouts, channelize(): frames = voltages.reshape(rows, 2, frames_n, chans)  5.32 us
    pallas_call x1, Pallas kernels, synthesize(): pl.pallas_call(functools.partial(voice_kernel, spectra_n, count, frames_n...  5.29 us
    transpose x1, local copies, waits for them, and re-layouts, synthesize(): jnp.transpose(bank, (4, 1, 3, 0, 2)).reshape(spectra_n, count, 2 * chans)  3.76 us
    unnamed x11, local copies, waits for them, and re-layouts  2.79 us

commit v1 on v0

v1 whole, which is shorter than its diff:
```python
import functools
import math

import jax
import jax.numpy as jnp
from jax import lax
from jax.experimental import pallas as pl
from jax.experimental.pallas import tpu as pltpu
from jax.sharding import PartitionSpec as P

NCH = 128
TAPS = 12
SPEC = 8
BLOCKS = 4
BEAMS = 256


def filter_table(taps, chans):
    length = taps.shape[0]
    position = jnp.arange(length, dtype=jnp.int32) % chans
    channel = jnp.arange(chans, dtype=jnp.int32)
    phase = (position[:, None] * channel[None, :] % chans).astype(jnp.float32) * (
        2.0 * math.pi / chans
    )
    cosine = taps[:, None] * jnp.cos(phase)
    sine = taps[:, None] * jnp.sin(phase)
    upper = jnp.concatenate([cosine, -sine], axis=1)
    lower = jnp.concatenate([sine, cosine], axis=1)
    return jnp.concatenate([upper, lower], axis=0).astype(jnp.bfloat16)


def resynthesize(received, table, taps_count, chans):
    count = received.shape[0]
    spectra_n = received.shape[3]
    table3 = table.reshape(2 * taps_count * chans, 2, chans)
    grid = jnp.einsum("pcht,mch->ptm", received, table3, preferred_element_type=jnp.float32)
    grid = grid.reshape(count, spectra_n, 2, taps_count, chans)
    total = jnp.zeros((count, spectra_n + taps_count - 1, 2, chans), jnp.float32)
    for k in range(taps_count):
        total = total + jnp.pad(
            grid[:, :, :, k, :], ((0, 0), (k, taps_count - 1 - k), (0, 0), (0, 0))
        )
    return jnp.transpose(total, (0, 2, 1, 3)).reshape(
        count, 2, (spectra_n + taps_count - 1) * chans
    )


def local_plain(voltages, taps, input_id, counts, delays, beam_owner):
    n_chan = lax.axis_size("chan")
    n_sub = lax.axis_size("sub")
    inp_dev = voltages.shape[0]
    inputs = input_id.shape[0]
    chans = NCH
    taps_count = TAPS
    spectra_n = BLOCKS * SPEC
    ch_dev = chans // n_chan
    rows = inputs // n_sub
    section = BEAMS // n_sub
    most = min(section, max(2, 2 * section // n_chan))
    table = filter_table(taps, chans)
    position = jnp.arange(spectra_n, dtype=jnp.int32)
    valid = (position % SPEC < jnp.repeat(counts, SPEC)).astype(jnp.float32)
    total = jnp.sum(counts.astype(jnp.float32))
    frames = voltages.reshape(inp_dev, 2, spectra_n + taps_count - 1, chans)
    windows = jnp.concatenate(
        [frames[:, :, k : k + spectra_n, :] for k in range(taps_count)], axis=3
    )
    table3 = table.reshape(2, taps_count * chans, 2 * chans)
    filtered = jnp.einsum("icth,chm->mit", windows, table3, preferred_element_type=jnp.float32)
    filtered = filtered * valid[None, None, :]
    spectra = filtered.reshape(2, chans, inp_dev, spectra_n).astype(jnp.bfloat16)
    slot_of = jnp.zeros((inputs,), jnp.int32).at[input_id].set(jnp.arange(inputs, dtype=jnp.int32))
    turned = lax.all_to_all(spectra, "chan", split_axis=1, concat_axis=2, tiled=True)
    gathered = lax.all_gather(turned, "sub", axis=2, tiled=True)
    chan_part = slot_of // (n_sub * inp_dev)
    sub_part = slot_of // inp_dev % n_sub
    order = (sub_part * n_chan + chan_part) * inp_dev + slot_of % inp_dev
    by_id = jnp.take(gathered, order, axis=2)
    sub_index = lax.axis_index("sub")
    mine = lax.dynamic_slice_in_dim(by_id, sub_index * rows, rows, 2)
    real_part = jnp.einsum("cxit,cxjt->xij", mine, by_id, preferred_element_type=jnp.float32)
    imag_part = jnp.einsum("xit,xjt->xij", mine[1], by_id[0], preferred_element_type=jnp.float32)
    imag_part = imag_part - jnp.einsum(
        "xit,xjt->xij", mine[0], by_id[1], preferred_element_type=jnp.float32
    )
    visibility = (jnp.stack([real_part, imag_part], axis=1) / total).astype(jnp.bfloat16)
    channel = lax.axis_index("chan") * ch_dev + jnp.arange(ch_dev, dtype=jnp.int32)
    phase = (delays[None, :, :] * channel[:, None, None] % chans).astype(jnp.float32) * (
        2.0 * math.pi / chans
    )
    scale = 1.0 / math.sqrt(inputs)
    weight_cos = (jnp.cos(phase) * scale).astype(jnp.bfloat16)
    weight_sin = (jnp.sin(phase) * scale).astype(jnp.bfloat16)
    from_cos = jnp.einsum("xbi,cxit->cxbt", weight_cos, by_id, preferred_element_type=jnp.float32)
    from_sin = jnp.einsum("xbi,cxit->cxbt", weight_sin, by_id, preferred_element_type=jnp.float32)
    beams = jnp.stack([from_cos[0] - from_sin[1], from_cos[1] + from_sin[0]]).astype(jnp.bfloat16)
    owner = lax.dynamic_slice_in_dim(beam_owner[:, 0], sub_index * section, section)
    beam = jnp.arange(section, dtype=jnp.int32)
    earlier = (owner[None, :] == owner[:, None]) & (beam[None, :] < beam[:, None])
    rank = jnp.sum(earlier.astype(jnp.int32), axis=1)
    target = owner * most + rank
    select = (jnp.arange(n_chan * most, dtype=jnp.int32)[:, None] == target[None, :]).astype(
        jnp.bfloat16
    )
    placed = jnp.einsum("pb,cxbt->pcxt", select, beams, preferred_element_type=jnp.float32).astype(
        jnp.bfloat16
    )
    placed = placed.reshape(n_chan, most, 2, ch_dev, spectra_n)
    resynth = resynthesize(
        lax.all_to_all(placed, "chan", split_axis=0, concat_axis=3, tiled=True)[0],
        table,
        taps_count,
        chans,
    )
    return (visibility, resynth)


def turn_of(steps):
    quarter = NCH // 4
    turn = steps & (NCH - 1)
    quadrant = (turn + quarter // 2) >> (quarter.bit_length() - 1)
    x = (turn - quadrant * quarter).astype(jnp.float32) * (2.0 * math.pi / NCH)
    y = x * x
    even = 1.0 + y * (-1 / 2 + y * (1 / 24 + y * (-1 / 720 + y * (1 / 40320))))
    odd = x * (1.0 + y * (-1 / 6 + y * (1 / 120 + y * (-1 / 5040 + y * (1 / 362880)))))
    swap = (quadrant & 1) == 1
    cosine, sine = jnp.where(swap, odd, even), jnp.where(swap, even, odd)
    cosine = jnp.where(((quadrant + 1) & 2) == 2, -cosine, cosine)
    return cosine, jnp.where((quadrant & 2) == 2, -sine, sine)


def weigh(first, scale, delay_ref, out_ref, at, left, high, wide):
    beams_n = delay_ref.shape[0]
    delay = delay_ref[at : at + high, left : left + wide]
    step_cos, step_sin = turn_of(delay)
    cosine, sine = turn_of(delay * first)

    def body(f, held):
        cosine, sine = held
        out_ref[f, at : at + high, left : left + wide] = cosine.astype(jnp.bfloat16)
        low = at + beams_n
        out_ref[f, low : low + high, left : left + wide] = sine.astype(jnp.bfloat16)
        return (
            cosine * step_cos - sine * step_sin,
            sine * step_cos + cosine * step_sin,
        )

    lax.fori_loop(0, out_ref.shape[0], body, (cosine * scale, sine * scale))


QUAD = 4


def trig_of(shape, n_grp):
    row = lax.broadcasted_iota(jnp.int32, shape, 0)
    lane = lax.broadcasted_iota(jnp.int32, shape, 1)
    tile = 2 * QUAD
    part = row // QUAD % 2
    channel = row // tile * QUAD + row % QUAD
    to_part = lane // NCH
    cosine, sine = turn_of(channel * (lane % NCH))
    return jnp.where(part == to_part, cosine, jnp.where(to_part == 1, sine, -sine))


def partner(x, lanes):
    pieces = [x[:, at : at + 128] for at in range(0, lanes, 128)]
    after = jnp.concatenate([pltpu.roll(p, 128 - QUAD, 1) for p in pieces], axis=1)
    before = jnp.concatenate([pltpu.roll(p, QUAD, 1) for p in pieces], axis=1)
    lane = lax.broadcasted_iota(jnp.int32, x.shape, 1)
    return lane // QUAD % 2 == 0, after, before


def front_kernel(
    n_chan, n_sub, most,
    frames_ref, taps_ref, counts_ref, names_ref, delay_ref, slot_ref,
    sorted_ref, beams_ref,
    x_ref, g_ref, y_ref, d_ref, perm_ref, c_ref, held, weight_ref, place_ref, ready,
    own_sem, out_sem, keep_sem, zs, zr, xs, xr, cs, cr, es, er,
):
    me_c, me_s = lax.axis_index("chan"), lax.axis_index("sub")
    core, across = me_s % 2, me_s // 2
    n_x = n_sub // 2
    twin = me_s + 1 - 2 * core
    mesh_id = pl.DeviceIdType.MESH
    pieces, per = x_ref.shape[1], x_ref.shape[2]
    n_grp = pieces * per
    spectra_n = BLOCKS * SPEC
    rows = frames_ref.shape[2]
    inputs = names_ref.shape[1]
    beams_n = delay_ref.shape[0]
    ch_dev = n_grp * QUAD
    tile = 2 * QUAD
    wide = 2 * NCH
    block = x_ref.shape[3]

    def chan_of(offset):
        return (me_c + offset) % n_chan

    def sub_of(offset):
        return (across + offset) % n_x * 2 + core

    barrier = pltpu.get_barrier_semaphore()
    for j in range(1, n_chan):
        pl.semaphore_signal(barrier, device_id={"chan": chan_of(j)}, device_id_type=mesh_id)
    for j in range(1, n_x):
        pl.semaphore_signal(barrier, device_id={"sub": sub_of(j)}, device_id_type=mesh_id)
    pl.semaphore_signal(barrier, device_id={"sub": twin}, device_id_type=mesh_id)

    def z_copy(j, q):
        return pltpu.make_async_remote_copy(
            src_ref=x_ref.at[chan_of(j), q],
            dst_ref=g_ref.at[q, me_c, me_s],
            send_sem=zs.at[j, q],
            recv_sem=zr.at[j, q],
            device_id={"chan": chan_of(j)},
            device_id_type=mesh_id,
        )

    def source(j, q):
        if j == 0:
            return x_ref.at[me_c, q]
        return g_ref.at[q, chan_of(n_chan - j), me_s]

    def x_copy(dx, j, q):
        return pltpu.make_async_remote_copy(
            src_ref=source(j, q),
            dst_ref=g_ref.at[q, chan_of(n_chan - j), me_s],
            send_sem=xs.at[dx, j, q],
            recv_sem=xr.at[dx, j, q],
            device_id={"sub": sub_of(dx)},
            device_id_type=mesh_id,
        )

    def core_copy(dx, j, q):
        home = g_ref.at[q, chan_of(n_chan - j), sub_of(n_x - dx)]
        return pltpu.make_async_remote_copy(
            src_ref=source(j, q) if dx == 0 else home,
            dst_ref=home,
            send_sem=cs.at[dx, j, q],
            recv_sem=cr.at[dx, j, q],
            device_id={"sub": twin},
            device_id_type=mesh_id,
        )

    def beam_copy(j, q):
        return pltpu.make_async_remote_copy(
            src_ref=ready.at[chan_of(j), q],
            dst_ref=beams_ref.at[me_c, q],
            send_sem=es.at[j, q],
            recv_sem=er.at[j, q],
            device_id={"chan": chan_of(j)},
            device_id_type=mesh_id,
        )

    trig = trig_of((n_chan * n_grp * tile, wide), n_grp)
    high = trig.astype(jnp.bfloat16)
    d_ref[:, :wide] = high
    d_ref[:, wide:] = (trig - high.astype(jnp.float32)).astype(jnp.bfloat16)

    valid = []
    for t in range(spectra_n):
        valid.append(jnp.where(counts_ref[t // SPEC] > t % SPEC, 1.0, 0.0))
    step = 16
    run = 4

    for c in range(2):

        @pl.loop(0, rows // step)
        def _(it):
            at = pl.multiple_of(it * step, step)
            taps = [taps_ref[k : k + 1, :] for k in range(TAPS)]
            for first in range(0, spectra_n, run):
                window = [
                    frames_ref[c, s, pl.ds(at, step), :].astype(jnp.float32)
                    for s in range(first, first + run + TAPS - 1)
                ]
                for j in range(run):
                    t = first + j
                    total = window[j] * taps[0]
                    for k in range(1, TAPS):
                        total = total + window[j + k] * taps[k]
                    total = total * valid[t]
                    high = total.astype(jnp.bfloat16)
                    low = (total - high.astype(jnp.float32)).astype(jnp.bfloat16)
                    slot = t // 2 * 2 + (t % 2 + core) % 2
                    to = pl.multiple_of(slot * rows + at, step)
                    y_ref[pl.ds(to, step), c * NCH : (c + 1) * NCH] = high
                    y_ref[pl.ds(to, step), wide + c * NCH : wide + (c + 1) * NCH] = low

    across_dims = (((1,), (1,)), ((), ()))

    @pl.loop(0, spectra_n // 4)
    def _(u):
        at = pl.multiple_of(u * 4 * rows, 4 * rows)
        high = y_ref[pl.ds(at, 4 * rows), :wide]
        low = y_ref[pl.ds(at, 4 * rows), wide:]
        out = lax.dot_general(d_ref[:, :wide], high, across_dims, preferred_element_type=jnp.float32)
        out = out + lax.dot_general(
            d_ref[:, wide:], high, across_dims, preferred_element_type=jnp.float32
        )
        out = out + lax.dot_general(
            d_ref[:, :wide], low, across_dims, preferred_element_type=jnp.float32
        )
        to = pl.multiple_of(u * 2 * tile, 2 * tile)
        for d in range(n_chan):
            for q in range(pieces):
                for e in range(per):
                    row = ((d * pieces + q) * per + e) * tile
                    both = jnp.concatenate(
                        [out[row : row + tile, :128], out[row : row + tile, 128:]], axis=0
                    )
                    x_ref[d, q, e, pl.ds(to, 2 * tile), :] = both.astype(jnp.bfloat16)

    pl.semaphore_wait(barrier, n_chan + n_x - 1)
    started = []

    def send(copy):
        copy.start()
        started.append(copy)

    def spread(j, q):
        for dx in range(1, n_x):
            send(x_copy(dx, j, q))
        send(core_copy(0, j, q))

    for q in range(pieces):
        for j in range(1, n_chan):
            send(z_copy(j, q))
    for q in range(pieces):
        spread(0, q)
    keeps = []
    for q in range(pieces):
        keep = pltpu.make_async_copy(x_ref.at[me_c, q], g_ref.at[q, me_c, me_s], keep_sem.at[q])
        keep.start()
        keeps.append(keep)

    half = inputs // 4
    first = me_c * ch_dev
    scale = 1.0 / math.sqrt(inputs)

    def name_unit(parity, m):
        def run_unit():
            name = names_ref[parity : parity + 1, :]
            low = lax.broadcasted_iota(jnp.int32, (half, inputs), 0) + m * half
            perm_ref[parity, m * half : (m + 1) * half, :] = jnp.where(
                name == low, 1.0, 0.0
            ).astype(jnp.bfloat16)

        return run_unit

    def weigh_unit(at, left):
        return lambda: weigh(first, scale, delay_ref, weight_ref, at, left, 16, 512)

    def place_unit():
        slots = place_ref.shape[1]
        lane = lax.broadcasted_iota(jnp.int32, (beams_n, slots), 1)
        for m in range(4):
            for e in range(per):
                want = slot_ref[...] + (e * n_chan * 4 + m) * most
                at = (m * per + e) * beams_n
                place_ref[at : at + beams_n, :] = jnp.where(lane == want, 1.0, 0.0).astype(
                    jnp.bfloat16
                )

    def join_unit(q):
        def run_unit():
            left = lax.broadcasted_iota(jnp.int32, (block, 128), 1) < 64
            for e in range(per):
                for c in range(n_chan):
                    for x in range(n_x):
                        a = g_ref[q, c, 2 * x, e].astype(jnp.float32)
                        b = g_ref[q, c, 2 * x + 1, e].astype(jnp.float32)
                        at = (c * n_x + x) * 128
                        c_ref[0, e * block : (e + 1) * block, at : at + 128] = jnp.where(
                            left, a, b
                        ).astype(jnp.bfloat16)
                        c_ref[1, e * block : (e + 1) * block, at : at + 128] = jnp.where(
                            left, b, a
                        ).astype(jnp.bfloat16)

        return run_unit

    def sort_unit(q, parity, m):
        def run_unit():
            out = lax.dot_general(
                perm_ref[parity, m * half : (m + 1) * half, :],
                c_ref[parity],
                across_dims,
                preferred_element_type=jnp.float32,
            ).astype(jnp.bfloat16)
            for e in range(per):
                held[q * per + e, m * half : (m + 1) * half, parity * block : (parity + 1) * block] = out[
                    :, e * block : (e + 1) * block
                ]

        return run_unit

    mixes = {}

    def mix_unit(q, e):
        def run_unit():
            at = q * per + e
            lane = lax.broadcasted_iota(jnp.int32, (2 * beams_n, 2 * block), 1)
            total = None
            for f in range(QUAD):
                mixed = jnp.dot(
                    weight_ref[at * QUAD + f], held[at], preferred_element_type=jnp.float32
                )
                total = mixed if total is None else jnp.where(lane % QUAD == f, mixed, total)
            real, after, before = partner(total[beams_n:], 2 * block)
            mixes[q, e] = total[:beams_n] + jnp.where(real, -after, before)

        return run_unit

    def place_beams(q):
        def run_unit():
            both = jnp.concatenate([mixes.pop((q, e)) for e in range(per)], axis=0)
            turned = both.T
            parts = []
            for m in range(4):
                parity, u = m % 2, m // 2
                picks = [
                    turned[parity * block + v * 2 * tile + u * tile :][:tile]
                    for v in range(spectra_n // 4)
                ]
                parts.append(jnp.concatenate(picks, axis=0))
            lined = jnp.concatenate(parts, axis=1).astype(jnp.bfloat16)
            out = jnp.dot(lined, place_ref[...], preferred_element_type=jnp.float32).astype(
                jnp.bfloat16
            )
            for e in range(per):
                for d in range(n_chan):
                    at = (e * n_chan + d) * 128
                    ready[d, q, e] = out[:, at : at + 128]
            for j in range(1, n_chan):
                send(beam_copy(j, q))
            keep = pltpu.make_async_copy(ready.at[me_c, q], beams_ref.at[me_c, q], own_sem.at[q])
            keep.start()
            keeps.append(keep)

        return run_unit

    def store_unit(q):
        def run_unit():
            part = pl.ds(q * per, per)
            keep = pltpu.make_async_copy(held.at[part], sorted_ref.at[part], out_sem.at[q])
            keep.start()
            keeps.append(keep)

        return run_unit

    def units_of(q):
        units = [join_unit(q)]
        units += [sort_unit(q, parity, m) for parity in range(2) for m in range(4)]
        units += [store_unit(q)] + [mix_unit(q, e) for e in range(per)] + [place_beams(q)]
        return units

    def z_step(j, q):
        def run_step():
            z_copy(j, q).wait_recv()
            spread(j, q)

        return run_step

    def x_step(j, q):
        for dx in range(1, n_x):
            x_copy(dx, j, q).wait_recv()
            send(core_copy(dx, j, q))

    def weave(units, steps):
        done = 0
        for i, one in enumerate(steps):
            upto = len(units) * (i + 1) // len(steps)
            for unit in units[done:upto]:
                unit()
            done = upto
            one()
        for unit in units[done:]:
            unit()

    def arrive(q):
        keeps[q].wait()
        for j in range(n_chan):
            for dx in range(n_x):
                core_copy(dx, j, q).wait_recv()

    setup = [name_unit(parity, m) for parity in range(2) for m in range(4)]
    setup += [
        weigh_unit(at, left) for at in range(0, beams_n, 16) for left in range(0, inputs, 512)
    ]
    setup.append(place_unit)
    weave(setup, [z_step(j, 0) for j in range(1, n_chan)])
    for q in range(1, pieces + 1):
        for j in range(n_chan):
            x_step(j, q - 1)
        arrive(q - 1)
        steps = [z_step(j, q) for j in range(1, n_chan)] if q < pieces else []
        weave(units_of(q - 1), steps)
    for q in range(pieces):
        for j in range(1, n_chan):
            beam_copy(j, q).wait_recv()
    for copy in started:
        copy.wait_send()
    for keep in keeps[pieces:]:
        keep.wait()


def front(frames, taps, counts, names, delays, slots, n_chan, n_sub, most):
    rows = frames.shape[2]
    beams_n, inputs = delays.shape
    spectra_n = BLOCKS * SPEC
    ch_dev = NCH // n_chan
    n_grp = ch_dev // QUAD
    per = 2
    pieces = n_grp // per
    n_x = n_sub // 2
    tile = 2 * QUAD
    block = spectra_n // 2 * tile
    dma = pltpu.SemaphoreType.DMA
    vmem = pl.BlockSpec(memory_space=pltpu.VMEM)
    travel = (n_chan, pieces, per, spectra_n // 4 * tile, 128)
    return pl.pallas_call(
        functools.partial(front_kernel, n_chan, n_sub, most),
        in_specs=[vmem, vmem, pl.BlockSpec(memory_space=pltpu.SMEM), vmem, vmem, vmem],
        out_specs=[pl.BlockSpec(memory_space=pl.ANY)] * 2,
        out_shape=[
            jax.ShapeDtypeStruct((n_grp, inputs, 2 * block), jnp.bfloat16),
            jax.ShapeDtypeStruct(travel, jnp.bfloat16),
        ],
        scratch_shapes=[
            pltpu.VMEM((n_chan, pieces, per, block, 128), jnp.bfloat16),
            pltpu.VMEM((pieces, n_chan, n_sub, per, block, 128), jnp.bfloat16),
            pltpu.VMEM((spectra_n * rows, 4 * NCH), jnp.bfloat16),
            pltpu.VMEM((2 * NCH, 4 * NCH), jnp.bfloat16),
            pltpu.VMEM((2, inputs, inputs), jnp.bfloat16),
            pltpu.VMEM((2, per * block, inputs), jnp.bfloat16),
            pltpu.VMEM((n_grp, inputs, 2 * block), jnp.bfloat16),
            pltpu.VMEM((ch_dev, 2 * beams_n, inputs), jnp.bfloat16),
            pltpu.VMEM((4 * per * beams_n, per * n_chan * 128), jnp.bfloat16),
            pltpu.VMEM(travel, jnp.bfloat16),
            dma((pieces,)),
            dma((pieces,)),
            dma((pieces,)),
            dma((n_chan, pieces)),
            dma((n_chan, pieces)),
            dma((n_x, n_chan, pieces)),
            dma((n_x, n_chan, pieces)),
            dma((n_x, n_chan, pieces)),
            dma((n_x, n_chan, pieces)),
            dma((n_chan, pieces)),
            dma((n_chan, pieces)),
        ],
        compiler_params=pltpu.CompilerParams(collective_id=0, has_side_effects=True),
        name="front",
    )(frames, taps, counts, names, delays, slots)


def back_kernel(
    per, sub_ref, counts_ref, mine_ref, all_ref, beams_ref, taps_ref,
    out_ref, voice_ref,
    turned_ref, bank_ref, table_ref,
):
    g, part = pl.program_id(0), pl.program_id(1)
    step = g * pl.num_programs(1) + part
    rows, lanes = mine_ref.shape[1], mine_ref.shape[2]
    inputs = all_ref.shape[1]
    count, _, samples = voice_ref.shape
    frames_n = samples // NCH
    spectra_n = frames_n - TAPS + 1
    n_chan, n_grp = beams_ref.shape[0], beams_ref.shape[1]
    tile = 2 * QUAD
    total = counts_ref[0]
    for i in range(1, BLOCKS):
        total = total + counts_ref[i]
    scale = 1.0 / jnp.full((8, 128), total.astype(jnp.float32))
    scale = scale[:1, :1]

    @pl.when(part == 0)
    def _():
        wide = mine_ref[0].astype(jnp.float32)
        real, after, before = partner(wide, lanes)
        turned_ref[...] = jnp.where(real, after, -before).astype(jnp.bfloat16)

    lane = lax.broadcasted_iota(jnp.int32, (rows, lanes), 1) % QUAD
    plain, turned = mine_ref[0].astype(jnp.float32), turned_ref[...].astype(jnp.float32)
    lefts = []
    for i in range(per):
        keep = lane == part * per + i
        lefts.append(jnp.where(keep, plain, 0.0).astype(jnp.bfloat16))
        lefts.append(jnp.where(keep, turned, 0.0).astype(jnp.bfloat16))
    left = jnp.concatenate(lefts, axis=0)
    for at in range(0, inputs, 256):
        product = lax.dot_general(
            left,
            all_ref[0, at : at + 256, :],
            (((1,), (1,)), ((), ())),
            preferred_element_type=jnp.float32,
        )
        product = (product * scale).astype(jnp.bfloat16)
        for i in range(per):
            for c in range(2):
                low = (2 * i + c) * rows
                out_ref[i, c, :, at : at + 256] = product[low : low + rows]

    @pl.when(step == 0)
    def _():
        edge = (TAPS - 1) * count
        bank_ref[:edge, :] = jnp.zeros((edge, 2 * NCH), jnp.bfloat16)
        end = edge + spectra_n * count
        bank_ref[end:, :] = jnp.zeros((bank_ref.shape[0] - end, 2 * NCH), jnp.bfloat16)
        for u in range(0, spectra_n // 4, 2):
            tiles = [
                beams_ref[c, e, u * tile : (u + 2) * tile, :].astype(jnp.float32)
                for c in range(n_chan)
                for e in range(n_grp)
            ]
            for v in range(2):
                stack = jnp.concatenate([t[v * tile : (v + 1) * tile] for t in tiles], axis=0)
                at = edge + (u + v) * 4 * count
                bank_ref[at : at + 4 * count, :] = stack.T.astype(jnp.bfloat16)

    @pl.when(step == 1)
    def _():
        trig = trig_of((2 * NCH, 2 * NCH), n_grp)
        for k in range(TAPS):
            taps = taps_ref[k : k + 1, :]
            table_ref[k] = (trig * jnp.concatenate([taps, taps], axis=1)).astype(jnp.bfloat16)

    run = 4
    chunk = step - 2

    @pl.when((chunk >= 0) & (chunk * run < frames_n))
    def _():
        acc = jnp.zeros((run * count, 2 * NCH), jnp.float32)
        for k in range(TAPS):
            start = pl.multiple_of((chunk * run - k + TAPS - 1) * count, count)
            acc = acc + jnp.dot(
                bank_ref[pl.ds(start, run * count), :],
                table_ref[k],
                preferred_element_type=jnp.float32,
            )
        for j in range(run):

            @pl.when(chunk * run + j < frames_n)
            def _():
                at = pl.multiple_of((chunk * run + j) * NCH, NCH)
                for c in range(2):
                    voice_ref[:, c, pl.ds(at, NCH)] = acc[
                        j * count : (j + 1) * count, c * NCH : (c + 1) * NCH
                    ]


def back(by_id, beams, taps, counts, sub_index, rows, count):
    n_grp, inputs, lanes = by_id.shape
    n_chan = beams.shape[0]
    beams = beams.reshape((n_chan, n_grp) + beams.shape[3:])
    spectra_n = BLOCKS * SPEC
    frames_n = spectra_n + TAPS - 1
    per = 2
    split = QUAD // per
    fixed = lambda shape: pl.BlockSpec(
        shape, lambda g, p, s: (0,) * len(shape), pipeline_mode=pl.Buffered(1)
    )
    return pl.pallas_call(
        functools.partial(back_kernel, per),
        grid_spec=pltpu.PrefetchScalarGridSpec(
            num_scalar_prefetch=1,
            grid=(n_grp, split),
            in_specs=[
                pl.BlockSpec(memory_space=pltpu.SMEM),
                pl.BlockSpec((1, rows, lanes), lambda g, p, s: (g, s[0], 0)),
                pl.BlockSpec((1, inputs, lanes), lambda g, p, s: (g, 0, 0)),
                fixed(beams.shape),
                fixed(taps.shape),
            ],
            out_specs=[
                pl.BlockSpec((per, 2, rows, inputs), lambda g, p, s: (g * split + p, 0, 0, 0)),
                fixed((count, 2, frames_n * NCH)),
            ],
            scratch_shapes=[
                pltpu.VMEM((rows, lanes), jnp.bfloat16),
                pltpu.VMEM(((spectra_n + 2 * TAPS) * count, 2 * NCH), jnp.bfloat16),
                pltpu.VMEM((TAPS, 2 * NCH, 2 * NCH), jnp.bfloat16),
            ],
        ),
        out_shape=[
            jax.ShapeDtypeStruct((n_grp * QUAD, 2, rows, inputs), jnp.bfloat16),
            jax.ShapeDtypeStruct((count, 2, frames_n * NCH), jnp.float32),
        ],
        compiler_params=pltpu.CompilerParams(dimension_semantics=("arbitrary", "arbitrary")),
        name="back",
    )(sub_index, counts, by_id, by_id, beams, taps)


def local(voltages, taps, input_id, counts, delays, beam_owner):
    n_chan = lax.axis_size("chan")
    n_sub = lax.axis_size("sub")
    inp_dev = voltages.shape[0]
    inputs = input_id.shape[0]
    spectra_n = BLOCKS * SPEC
    ch_dev = NCH // n_chan
    rows = inputs // n_sub
    section = BEAMS // n_sub
    most = min(section, max(2, 2 * section // n_chan))
    fits = inp_dev == 64 and most == 32 and section == 64 and NCH == 128
    fits = fits and n_sub % 2 == 0 and ch_dev % (2 * QUAD) == 0 and inputs % 512 == 0
    if not fits or 4 * ch_dev * QUAD < 11 + 2 * QUAD or rows % 128:
        return local_plain(voltages, taps, input_id, counts, delays, beam_owner)
    sub_index = lax.axis_index("sub")
    frames = voltages.reshape(inp_dev, 2, spectra_n + TAPS - 1, NCH)
    frames = jnp.transpose(frames, (1, 2, 0, 3))
    swapped = input_id.reshape(-1, 2, inp_dev)[:, ::-1].reshape(inputs)
    names = jnp.stack([input_id, swapped])
    owner = lax.dynamic_slice_in_dim(beam_owner[:, 0], sub_index * section, section)
    beam = jnp.arange(section, dtype=jnp.int32)
    earlier = (owner[None, :] == owner[:, None]) & (beam[None, :] < beam[:, None])
    rank = jnp.sum(earlier.astype(jnp.int32), axis=1)
    slots = (owner * (4 * most) + rank)[:, None]
    taps2 = taps.reshape(TAPS, NCH)
    by_id, beams = front(frames, taps2, counts, names, delays, slots, n_chan, n_sub, most)
    visibility, resynth = back(
        by_id, beams, taps2, counts, sub_index.astype(jnp.int32)[None], rows, most
    )
    return (visibility, resynth)


def solution(mesh):
    placed = (
        P(("grp", "chan", "sub"), None, None),
        P(),
        P(),
        P("grp"),
        P(("grp", "sub"), None),
        P("grp", None),
    )
    return jax.shard_map(
        local,
        mesh=mesh,
        in_specs=placed,
        out_specs=(P(("grp", "chan"), None, "sub", None), P(("grp", "chan", "sub"), None, None)),
        check_vma=False,
    )
```

time: 133 us -> 94.2 us (0.71)
  Pallas kernels: 104 us -> 83.5 us
  other arithmetic: 11.9 us -> 2.09 us
  local copies, waits for them, and re-layouts: 14.3 us -> 7.21 us
    pallas_call x5 -> x2, Pallas kernels: 104 us -> 83.5 us  [the longest x1 57.5 us: front(): pl.pallas_call(functools.partial(front_kernel, n_chan, n_sub, most), in_s...]
    convert_element_type x5 -> x0, other arithmetic: 6.24 us -> none  [the longest x1 2.28 us: channelize(): weights = (trig[None] * factor).astype(jnp.bfloat16)]
    select_n x4 -> x0, other arithmetic: 4.04 us -> none  [the longest x1 2.21 us: channelize(): jnp.where(lower == (part[None, :] == 1), cosine, jnp.where(lower, sine, -...]
    transpose x2 -> x0, local copies, waits for them, and re-layouts: 3.77 us -> none  [the longest x1 3.76 us: synthesize(): jnp.transpose(bank, (4, 1, 3, 0, 2)).reshape(spectra_n, count, 2 * chans)]
    unnamed x11 -> x3, local copies, waits for them, and re-layouts: 2.79 us -> 0.77 us
    reshape x5 -> x3, local copies, waits for them, and re-layouts: 6.32 us -> 6.08 us  [the longest x2 5.31 us: local(): frames = voltages.reshape(inp_dev, 2, spectra_n + TAPS - 1, NCH)]
where the time goes in v1:
time: 94.2 us; the launch traced here: 93.5 us
  Pallas kernels  83.5 us (89%)
  local copies, waits for them, and re-layouts  7.21 us (8%)
  other arithmetic  2.09 us (2%)
    pallas_call x1, Pallas kernels, front(): pl.pallas_call(functools.partial(front_kernel, n_chan, n_sub, most), in_s...  57.5 us
    pallas_call x1, Pallas kernels, back(): pl.pallas_call(functools.partial(back_kernel, per), grid_spec=pltpu.Prefe...  26 us
    reshape x2, local copies, waits for them, and re-layouts, local(): frames = voltages.reshape(inp_dev, 2, spectra_n + TAPS - 1, NCH)  5.31 us

profile of v1, /device:TPU:0, one launch (start us, length us, event | category | flops | bytes accessed | tf_op | source)
XLA Modules:
  0.0 93.5 jit_solution(17168630245815358699)
XLA Ops:
  0.6 0.0 copy-start
  0.6 0.7 copy-done
  1.3 0.1 fusion.1
  1.4 0.1 constant_dynamic-slice_fusion
  1.5 0.2 convert_reduce_fusion
  1.6 0.8 reshape.23
  2.4 0.1 stack_reshape.3
  2.5 1.3 %pad_add_fusion.names_ref = s32[2,1024]{1,0:T(2,128)} fusion(s32[1,1024]{1,0:T(1,128)S(1)} %stack_reshape.3, s32[1,1024]{1,0:T(1,128)} %bitcast.14), kind=kLoop, calls=%fused_computation.5 | loop fusion | flops 2048 | bytes 16384 | tf_op jit(solution)/shard_map/stack | solution.py:713
  3.8 0.1 copy.22
  3.9 0.1 copy.25
  4.0 0.6 multiply_add_fusion.slot_ref
  4.6 3.7 %reshape.25 = bf16[64,2,43,128]{3,2,1,0:T(8,128)(2,1)S(1)} reshape(bf16[64,2,5504]{2,1,0:T(2,128)(2,1)} %param.6) | data formatting | bytes 2818048 | tf_op jit(solution)/shard_map/reshape | solution.py:710
  8.3 1.6 %copy.28 = bf16[64,2,43,128]{3,0,2,1:T(8,128)(2,1)} copy(bf16[64,2,43,128]{3,2,1,0:T(8,128)(2,1)S(1)} %reshape.25) | data formatting | bytes 2818048 | tf_op jit(solution)/shard_map/reshape | solution.py:710
  10.0 57.5 %front.1 = (bf16[8,1024,256]{2,1,0:T(8,128)(2,1)}, bf16[4,4,2,64,128]{4,3,2,1,0:T(8,128)(2,1)}) custom-call(bf16[2,43,64,128]{3,2,1,0:T(8,128)(2,1)} %bitcast.10, f32[12,128]{1,0:T(8,128)} %bitcast.12, s32[4]{0:T(128)} %counts_ref.3, s32[2,1024]{1,0:T(2,128)} %pad_add_fusion.names_ref, s32[64,1024]{1,0:T(8,128)} %delay_ref.1, s32[64,1]{1,0:T(8,128)} %multiply_add_fusion.slot_ref), custom_call_target="tpu_custom_call" | custom-call | tf_op jit(solution)/shard_map/front/pallas_call | solution.py:522
  67.5 26.0 %back.1 = (bf16[32,2,256,1024]{3,2,1,0:T(8,128)(2,1)}, f32[32,2,5504]{2,1,0:T(2,128)}) custom-call(s32[1]{0:T(128)} %bitcast.sub_ref, s32[4]{0:T(128)} %counts_ref.3, bf16[8,1024,256]{2,1,0:T(8,128)(2,1)} %get-tuple-element.4.mine_ref.all_ref, bf16[8,1024,256]{2,1,0:T(8,128)(2,1)} %get-tuple-element.4.mine_ref.all_ref, bf16[4,8,64,128]{3,2,1,0:T(8,128)(2,1)} %bitcast.11, ...), custom_call_target="tpu_custom_call" | custom-call | tf_op jit(solution)/shard_map/back/pallas_call | solution.py:664
  (1 shorter events, 0.0 us)
Async XLA Ops:
  0.6 0.7 copy-start

commit v2 on v1

--- a/solution.py
+++ b/solution.py
@@ -149,6 +149,7 @@
 
 
 QUAD = 4
+VOICES = 8
 
 
 def trig_of(shape, n_grp):
@@ -172,10 +173,11 @@
 
 def front_kernel(
     n_chan, n_sub, most,
-    frames_ref, taps_ref, counts_ref, names_ref, delay_ref, slot_ref,
+    volt_ref, taps_ref, counts_ref, name_ref, delay_ref, owner_ref,
     sorted_ref, beams_ref,
-    x_ref, g_ref, y_ref, d_ref, perm_ref, c_ref, held, weight_ref, place_ref, ready,
-    own_sem, out_sem, keep_sem, zs, zr, xs, xr, cs, cr, es, er,
+    v_ref, late_ref, x_ref, g_ref, y_ref, d_ref, perm_ref, turn_ref, c_ref, held, weight_ref,
+    place_ref, ready,
+    load_sem, own_sem, out_sem, keep_sem, zs, zr, xs, xr, cs, cr, es, er,
 ):
     me_c, me_s = lax.axis_index("chan"), lax.axis_index("sub")
     core, across = me_s % 2, me_s // 2
@@ -185,8 +187,8 @@
     pieces, per = x_ref.shape[1], x_ref.shape[2]
     n_grp = pieces * per
     spectra_n = BLOCKS * SPEC
-    rows = frames_ref.shape[2]
-    inputs = names_ref.shape[1]
+    frames_n, rows = v_ref.shape[:2]
+    inputs = name_ref.shape[1]
     beams_n = delay_ref.shape[0]
     ch_dev = n_grp * QUAD
     tile = 2 * QUAD
@@ -206,12 +208,17 @@
         pl.semaphore_signal(barrier, device_id={"sub": sub_of(j)}, device_id_type=mesh_id)
     pl.semaphore_signal(barrier, device_id={"sub": twin}, device_id_type=mesh_id)
 
+    for s in range(frames_n):
+        pltpu.make_async_copy(
+            volt_ref.at[:, :, pl.ds(s * NCH, NCH)], v_ref.at[s], load_sem
+        ).start()
+
     def z_copy(j, q):
         return pltpu.make_async_remote_copy(
             src_ref=x_ref.at[chan_of(j), q],
             dst_ref=g_ref.at[q, me_c, me_s],
-            send_sem=zs.at[j, q],
-            recv_sem=zr.at[j, q],
+            send_sem=zs,
+            recv_sem=zr.at[j - 1, q],
             device_id={"chan": chan_of(j)},
             device_id_type=mesh_id,
         )
@@ -225,8 +232,8 @@
         return pltpu.make_async_remote_copy(
             src_ref=source(j, q),
             dst_ref=g_ref.at[q, chan_of(n_chan - j), me_s],
-            send_sem=xs.at[dx, j, q],
-            recv_sem=xr.at[dx, j, q],
+            send_sem=xs,
+            recv_sem=xr.at[dx - 1, j, q],
             device_id={"sub": sub_of(dx)},
             device_id_type=mesh_id,
         )
@@ -236,8 +243,8 @@
         return pltpu.make_async_remote_copy(
             src_ref=source(j, q) if dx == 0 else home,
             dst_ref=home,
-            send_sem=cs.at[dx, j, q],
-            recv_sem=cr.at[dx, j, q],
+            send_sem=cs,
+            recv_sem=cr.at[q],
             device_id={"sub": twin},
             device_id_type=mesh_id,
         )
@@ -246,8 +253,8 @@
         return pltpu.make_async_remote_copy(
             src_ref=ready.at[chan_of(j), q],
             dst_ref=beams_ref.at[me_c, q],
-            send_sem=es.at[j, q],
-            recv_sem=er.at[j, q],
+            send_sem=es,
+            recv_sem=er,
             device_id={"chan": chan_of(j)},
             device_id_type=mesh_id,
         )
@@ -262,16 +269,18 @@
         valid.append(jnp.where(counts_ref[t // SPEC] > t % SPEC, 1.0, 0.0))
     step = 16
     run = 4
-
-    for c in range(2):
-
-        @pl.loop(0, rows // step)
-        def _(it):
-            at = pl.multiple_of(it * step, step)
-            taps = [taps_ref[k : k + 1, :] for k in range(TAPS)]
+    pltpu.make_async_copy(v_ref, v_ref, load_sem).wait()
+
+    @pl.loop(0, rows // step)
+    def _(it):
+        at = pl.multiple_of(it * step, step)
+        taps = [taps_ref[k : k + 1, :] for k in range(TAPS)]
+        for h in range(2):
             for first in range(0, spectra_n, run):
                 window = [
-                    frames_ref[c, s, pl.ds(at, step), :].astype(jnp.float32)
+                    v_ref[s, pl.ds(at + h * (step // 2), step // 2)]
+                    .reshape(step, NCH)
+                    .astype(jnp.float32)
                     for s in range(first, first + run + TAPS - 1)
                 ]
                 for j in range(run):
@@ -279,13 +288,16 @@
                     total = window[j] * taps[0]
                     for k in range(1, TAPS):
                         total = total + window[j + k] * taps[k]
-                    total = total * valid[t]
-                    high = total.astype(jnp.bfloat16)
-                    low = (total - high.astype(jnp.float32)).astype(jnp.bfloat16)
-                    slot = t // 2 * 2 + (t % 2 + core) % 2
-                    to = pl.multiple_of(slot * rows + at, step)
-                    y_ref[pl.ds(to, step), c * NCH : (c + 1) * NCH] = high
-                    y_ref[pl.ds(to, step), wide + c * NCH : wide + (c + 1) * NCH] = low
+                    late_ref[t, h * step : (h + 1) * step, :] = total * valid[t]
+        for t in range(spectra_n):
+            slot = t // 2 * 2 + (t % 2 + core) % 2
+            to = pl.multiple_of(slot * rows + at, step)
+            for c in range(2):
+                total = late_ref[t, pl.ds(c, step, stride=2), :]
+                high = total.astype(jnp.bfloat16)
+                low = (total - high.astype(jnp.float32)).astype(jnp.bfloat16)
+                y_ref[pl.ds(to, step), c * NCH : (c + 1) * NCH] = high
+                y_ref[pl.ds(to, step), wide + c * NCH : wide + (c + 1) * NCH] = low
 
     across_dims = (((1,), (1,)), ((), ()))
 
@@ -312,86 +324,91 @@
                     x_ref[d, q, e, pl.ds(to, 2 * tile), :] = both.astype(jnp.bfloat16)
 
     pl.semaphore_wait(barrier, n_chan + n_x - 1)
-    started = []
-
-    def send(copy):
-        copy.start()
-        started.append(copy)
-
     def spread(j, q):
         for dx in range(1, n_x):
-            send(x_copy(dx, j, q))
-        send(core_copy(0, j, q))
+            x_copy(dx, j, q).start()
+        core_copy(0, j, q).start()
 
     for q in range(pieces):
         for j in range(1, n_chan):
-            send(z_copy(j, q))
+            z_copy(j, q).start()
     for q in range(pieces):
         spread(0, q)
-    keeps = []
     for q in range(pieces):
-        keep = pltpu.make_async_copy(x_ref.at[me_c, q], g_ref.at[q, me_c, me_s], keep_sem.at[q])
-        keep.start()
-        keeps.append(keep)
+        pltpu.make_async_copy(x_ref.at[me_c, q], g_ref.at[q, me_c, me_s], keep_sem).start()
 
     half = inputs // 4
     first = me_c * ch_dev
     scale = 1.0 / math.sqrt(inputs)
 
-    def name_unit(parity, m):
+    def name_unit(m):
         def run_unit():
-            name = names_ref[parity : parity + 1, :]
             low = lax.broadcasted_iota(jnp.int32, (half, inputs), 0) + m * half
-            perm_ref[parity, m * half : (m + 1) * half, :] = jnp.where(
-                name == low, 1.0, 0.0
+            perm_ref[m * half : (m + 1) * half, :] = jnp.where(
+                name_ref[...] == low, 1.0, 0.0
             ).astype(jnp.bfloat16)
 
         return run_unit
 
+    def turn_unit():
+        turned = jnp.dot(
+            delay_ref[...].astype(jnp.float32).astype(jnp.bfloat16),
+            perm_ref[...],
+            preferred_element_type=jnp.float32,
+        )
+        turn_ref[...] = turned.astype(jnp.int32)
+
     def weigh_unit(at, left):
-        return lambda: weigh(first, scale, delay_ref, weight_ref, at, left, 16, 512)
+        return lambda: weigh(first, scale, turn_ref, weight_ref, at, left, 16, 512)
 
     def place_unit():
-        slots = place_ref.shape[1]
-        lane = lax.broadcasted_iota(jnp.int32, (beams_n, slots), 1)
+        lanes = per * beams_n
+        owner = jnp.concatenate([owner_ref[...]] * per, axis=1)
+        named = (lax.broadcasted_iota(jnp.int32, (8, lanes), 0) == owner).astype(jnp.float32)
+        row = lax.broadcasted_iota(jnp.int32, (lanes, lanes), 0)
+        lane = lax.broadcasted_iota(jnp.int32, (lanes, lanes), 1)
+        before = (row < lane) & (row // beams_n == lane // beams_n)
+        rank = jnp.dot(
+            named.astype(jnp.bfloat16),
+            jnp.where(before, 1.0, 0.0).astype(jnp.bfloat16),
+            preferred_element_type=jnp.float32,
+        )
+        rank = jnp.sum(named * rank, axis=0, keepdims=True).astype(jnp.int32)
+        lane = lax.broadcasted_iota(jnp.int32, (1, lanes), 1)
+        slot = (lane // beams_n * n_chan + owner) * (4 * most) + rank
+        row = lax.broadcasted_iota(jnp.int32, (place_ref.shape[0], lanes), 0)
         for m in range(4):
-            for e in range(per):
-                want = slot_ref[...] + (e * n_chan * 4 + m) * most
-                at = (m * per + e) * beams_n
-                place_ref[at : at + beams_n, :] = jnp.where(lane == want, 1.0, 0.0).astype(
-                    jnp.bfloat16
-                )
+            place_ref[:, m * lanes : (m + 1) * lanes] = jnp.where(
+                row == slot + m * most, 1.0, 0.0
+            ).astype(jnp.bfloat16)
 
     def join_unit(q):
         def run_unit():
             left = lax.broadcasted_iota(jnp.int32, (block, 128), 1) < 64
             for e in range(per):
+                low = 2 * e * block
                 for c in range(n_chan):
                     for x in range(n_x):
                         a = g_ref[q, c, 2 * x, e].astype(jnp.float32)
                         b = g_ref[q, c, 2 * x + 1, e].astype(jnp.float32)
                         at = (c * n_x + x) * 128
-                        c_ref[0, e * block : (e + 1) * block, at : at + 128] = jnp.where(
-                            left, a, b
+                        c_ref[low : low + block, at : at + 128] = jnp.where(left, a, b).astype(
+                            jnp.bfloat16
+                        )
+                        c_ref[low + block : low + 2 * block, at : at + 128] = pltpu.roll(
+                            jnp.where(left, b, a), 64, 1
                         ).astype(jnp.bfloat16)
-                        c_ref[1, e * block : (e + 1) * block, at : at + 128] = jnp.where(
-                            left, b, a
-                        ).astype(jnp.bfloat16)
 
         return run_unit
 
-    def sort_unit(q, parity, m):
+    def sort_unit(q, e, m):
         def run_unit():
-            out = lax.dot_general(
-                perm_ref[parity, m * half : (m + 1) * half, :],
-                c_ref[parity],
+            held[q * per + e, m * half : (m + 1) * half, :] = lax.dot_general(
+                perm_ref[m * half : (m + 1) * half, :],
+                c_ref[2 * e * block : 2 * (e + 1) * block, :],
                 across_dims,
                 preferred_element_type=jnp.float32,
             ).astype(jnp.bfloat16)
-            for e in range(per):
-                held[q * per + e, m * half : (m + 1) * half, parity * block : (parity + 1) * block] = out[
-                    :, e * block : (e + 1) * block
-                ]
 
         return run_unit
 
@@ -403,8 +420,11 @@
             lane = lax.broadcasted_iota(jnp.int32, (2 * beams_n, 2 * block), 1)
             total = None
             for f in range(QUAD):
-                mixed = jnp.dot(
-                    weight_ref[at * QUAD + f], held[at], preferred_element_type=jnp.float32
+                mixed = lax.dot_general(
+                    weight_ref[at * QUAD + f],
+                    c_ref[2 * e * block : 2 * (e + 1) * block, :],
+                    across_dims,
+                    preferred_element_type=jnp.float32,
                 )
                 total = mixed if total is None else jnp.where(lane % QUAD == f, mixed, total)
             real, after, before = partner(total[beams_n:], 2 * block)
@@ -425,35 +445,30 @@
                 ]
                 parts.append(jnp.concatenate(picks, axis=0))
             lined = jnp.concatenate(parts, axis=1).astype(jnp.bfloat16)
-            out = jnp.dot(lined, place_ref[...], preferred_element_type=jnp.float32).astype(
-                jnp.bfloat16
-            )
+            out = lax.dot_general(
+                lined, place_ref[...], across_dims, preferred_element_type=jnp.float32
+            ).astype(jnp.bfloat16)
             for e in range(per):
                 for d in range(n_chan):
                     at = (e * n_chan + d) * 128
                     ready[d, q, e] = out[:, at : at + 128]
             for j in range(1, n_chan):
-                send(beam_copy(j, q))
-            keep = pltpu.make_async_copy(ready.at[me_c, q], beams_ref.at[me_c, q], own_sem.at[q])
-            keep.start()
-            keeps.append(keep)
+                beam_copy(j, q).start()
+            pltpu.make_async_copy(ready.at[me_c, q], beams_ref.at[me_c, q], own_sem).start()
 
         return run_unit
 
     def store_unit(q):
         def run_unit():
             part = pl.ds(q * per, per)
-            keep = pltpu.make_async_copy(held.at[part], sorted_ref.at[part], out_sem.at[q])
-            keep.start()
-            keeps.append(keep)
+            pltpu.make_async_copy(held.at[part], sorted_ref.at[part], out_sem).start()
 
         return run_unit
 
     def units_of(q):
-        units = [join_unit(q)]
-        units += [sort_unit(q, parity, m) for parity in range(2) for m in range(4)]
-        units += [store_unit(q)] + [mix_unit(q, e) for e in range(per)] + [place_beams(q)]
-        return units
+        units = [join_unit(q)] + [mix_unit(q, e) for e in range(per)] + [place_beams(q)]
+        units += [sort_unit(q, e, m) for e in range(per) for m in range(4)]
+        return units + [store_unit(q)]
 
     def z_step(j, q):
         def run_step():
@@ -465,7 +480,7 @@
     def x_step(j, q):
         for dx in range(1, n_x):
             x_copy(dx, j, q).wait_recv()
-            send(core_copy(dx, j, q))
+            core_copy(dx, j, q).start()
 
     def weave(units, steps):
         done = 0
@@ -479,12 +494,12 @@
             unit()
 
     def arrive(q):
-        keeps[q].wait()
-        for j in range(n_chan):
-            for dx in range(n_x):
-                core_copy(dx, j, q).wait_recv()
-
-    setup = [name_unit(parity, m) for parity in range(2) for m in range(4)]
+        if q == 0:
+            pltpu.make_async_copy(x_ref.at[me_c], g_ref.at[:, me_c, me_s], keep_sem).wait()
+        part = g_ref.at[q, pl.ds(0, n_chan // 2)]
+        pltpu.make_async_copy(part, part, cr.at[q]).wait()
+
+    setup = [name_unit(m) for m in range(4)] + [turn_unit]
     setup += [
         weigh_unit(at, left) for at in range(0, beams_n, 16) for left in range(0, inputs, 512)
     ]
@@ -496,17 +511,20 @@
         arrive(q - 1)
         steps = [z_step(j, q) for j in range(1, n_chan)] if q < pieces else []
         weave(units_of(q - 1), steps)
-    for q in range(pieces):
-        for j in range(1, n_chan):
-            beam_copy(j, q).wait_recv()
-    for copy in started:
-        copy.wait_send()
-    for keep in keeps[pieces:]:
-        keep.wait()
-
-
-def front(frames, taps, counts, names, delays, slots, n_chan, n_sub, most):
-    rows = frames.shape[2]
+    others = pl.ds(0, n_chan - 1)
+    pltpu.make_async_copy(ready.at[others], beams_ref.at[others], er).wait()
+    pltpu.make_async_copy(x_ref.at[others], x_ref.at[others], zs).wait()
+    for dx in range(1, n_x):
+        pltpu.make_async_copy(x_ref, x_ref, xs).wait()
+    part = g_ref.at[pl.ds(0, pieces // 2)]
+    pltpu.make_async_copy(part, part, cs).wait()
+    pltpu.make_async_copy(ready.at[others], ready.at[others], es).wait()
+    pltpu.make_async_copy(ready.at[me_c], beams_ref.at[me_c], own_sem).wait()
+    pltpu.make_async_copy(held, sorted_ref, out_sem).wait()
+
+
+def front(voltages, taps, counts, names, delays, owner, n_chan, n_sub, most):
+    rows = voltages.shape[0]
     beams_n, inputs = delays.shape
     spectra_n = BLOCKS * SPEC
     ch_dev = NCH // n_chan
@@ -521,49 +539,60 @@
     travel = (n_chan, pieces, per, spectra_n // 4 * tile, 128)
     return pl.pallas_call(
         functools.partial(front_kernel, n_chan, n_sub, most),
-        in_specs=[vmem, vmem, pl.BlockSpec(memory_space=pltpu.SMEM), vmem, vmem, vmem],
+        in_specs=[
+            pl.BlockSpec(memory_space=pl.ANY),
+            vmem,
+            pl.BlockSpec(memory_space=pltpu.SMEM),
+            vmem,
+            vmem,
+            vmem,
+        ],
         out_specs=[pl.BlockSpec(memory_space=pl.ANY)] * 2,
         out_shape=[
             jax.ShapeDtypeStruct((n_grp, inputs, 2 * block), jnp.bfloat16),
             jax.ShapeDtypeStruct(travel, jnp.bfloat16),
         ],
         scratch_shapes=[
+            pltpu.VMEM((spectra_n + TAPS - 1, rows, 2, NCH), jnp.bfloat16),
+            pltpu.VMEM((spectra_n, 32, NCH), jnp.float32),
             pltpu.VMEM((n_chan, pieces, per, block, 128), jnp.bfloat16),
             pltpu.VMEM((pieces, n_chan, n_sub, per, block, 128), jnp.bfloat16),
             pltpu.VMEM((spectra_n * rows, 4 * NCH), jnp.bfloat16),
             pltpu.VMEM((2 * NCH, 4 * NCH), jnp.bfloat16),
-            pltpu.VMEM((2, inputs, inputs), jnp.bfloat16),
-            pltpu.VMEM((2, per * block, inputs), jnp.bfloat16),
+            pltpu.VMEM((inputs, inputs), jnp.bfloat16),
+            pltpu.VMEM((beams_n, inputs), jnp.int32),
+            pltpu.VMEM((2 * per * block, inputs), jnp.bfloat16),
             pltpu.VMEM((n_grp, inputs, 2 * block), jnp.bfloat16),
             pltpu.VMEM((ch_dev, 2 * beams_n, inputs), jnp.bfloat16),
-            pltpu.VMEM((4 * per * beams_n, per * n_chan * 128), jnp.bfloat16),
+            pltpu.VMEM((per * n_chan * 128, 4 * per * beams_n), jnp.bfloat16),
             pltpu.VMEM(travel, jnp.bfloat16),
+            dma,
+            dma,
+            dma,
+            dma,
+            dma,
+            dma((n_chan - 1, pieces)),
+            dma,
+            dma((n_x - 1, n_chan, pieces)),
+            dma,
             dma((pieces,)),
-            dma((pieces,)),
-            dma((pieces,)),
-            dma((n_chan, pieces)),
-            dma((n_chan, pieces)),
-            dma((n_x, n_chan, pieces)),
-            dma((n_x, n_chan, pieces)),
-            dma((n_x, n_chan, pieces)),
-            dma((n_x, n_chan, pieces)),
-            dma((n_chan, pieces)),
-            dma((n_chan, pieces)),
+            dma,
+            dma,
         ],
         compiler_params=pltpu.CompilerParams(collective_id=0, has_side_effects=True),
         name="front",
-    )(frames, taps, counts, names, delays, slots)
+    )(voltages, taps, counts, names, delays, owner)
 
 
 def back_kernel(
-    per, sub_ref, counts_ref, mine_ref, all_ref, beams_ref, taps_ref,
+    sub_ref, counts_ref, mine_ref, all_ref, beams_ref, taps_ref,
     out_ref, voice_ref,
-    turned_ref, bank_ref, table_ref,
+    left_ref, bank_ref, table_ref,
 ):
     g, part = pl.program_id(0), pl.program_id(1)
     step = g * pl.num_programs(1) + part
     rows, lanes = mine_ref.shape[1], mine_ref.shape[2]
-    inputs = all_ref.shape[1]
+    span = all_ref.shape[1]
     count, _, samples = voice_ref.shape
     frames_n = samples // NCH
     spectra_n = frames_n - TAPS + 1
@@ -577,27 +606,26 @@
 
     @pl.when(part == 0)
     def _():
-        wide = mine_ref[0].astype(jnp.float32)
-        real, after, before = partner(wide, lanes)
-        turned_ref[...] = jnp.where(real, after, -before).astype(jnp.bfloat16)
-
-    lane = lax.broadcasted_iota(jnp.int32, (rows, lanes), 1) % QUAD
-    plain, turned = mine_ref[0].astype(jnp.float32), turned_ref[...].astype(jnp.float32)
-    lefts = []
-    for i in range(per):
-        keep = lane == part * per + i
-        lefts.append(jnp.where(keep, plain, 0.0).astype(jnp.bfloat16))
-        lefts.append(jnp.where(keep, turned, 0.0).astype(jnp.bfloat16))
-    left = jnp.concatenate(lefts, axis=0)
-    for at in range(0, inputs, 256):
+        plain = mine_ref[0].astype(jnp.float32)
+        real, after, before = partner(plain, lanes)
+        turned = jnp.where(real, after, -before)
+        lane = lax.broadcasted_iota(jnp.int32, (rows, lanes), 1) % QUAD
+        for i in range(QUAD):
+            at = 2 * i * rows
+            left_ref[at : at + rows, :] = jnp.where(lane == i, plain, 0.0).astype(jnp.bfloat16)
+            left_ref[at + rows : at + 2 * rows, :] = jnp.where(lane == i, turned, 0.0).astype(
+                jnp.bfloat16
+            )
+
+    for at in range(0, span, 256):
         product = lax.dot_general(
-            left,
+            left_ref[...],
             all_ref[0, at : at + 256, :],
             (((1,), (1,)), ((), ())),
             preferred_element_type=jnp.float32,
         )
         product = (product * scale).astype(jnp.bfloat16)
-        for i in range(per):
+        for i in range(QUAD):
             for c in range(2):
                 low = (2 * i + c) * rows
                 out_ref[i, c, :, at : at + 256] = product[low : low + rows]
@@ -626,7 +654,7 @@
             taps = taps_ref[k : k + 1, :]
             table_ref[k] = (trig * jnp.concatenate([taps, taps], axis=1)).astype(jnp.bfloat16)
 
-    run = 4
+    run = VOICES
     chunk = step - 2
 
     @pl.when((chunk >= 0) & (chunk * run < frames_n))
@@ -656,30 +684,30 @@
     beams = beams.reshape((n_chan, n_grp) + beams.shape[3:])
     spectra_n = BLOCKS * SPEC
     frames_n = spectra_n + TAPS - 1
-    per = 2
-    split = QUAD // per
+    split = 2
+    span = inputs // split
     fixed = lambda shape: pl.BlockSpec(
         shape, lambda g, p, s: (0,) * len(shape), pipeline_mode=pl.Buffered(1)
     )
     return pl.pallas_call(
-        functools.partial(back_kernel, per),
+        back_kernel,
         grid_spec=pltpu.PrefetchScalarGridSpec(
             num_scalar_prefetch=1,
             grid=(n_grp, split),
             in_specs=[
                 pl.BlockSpec(memory_space=pltpu.SMEM),
                 pl.BlockSpec((1, rows, lanes), lambda g, p, s: (g, s[0], 0)),
-                pl.BlockSpec((1, inputs, lanes), lambda g, p, s: (g, 0, 0)),
+                pl.BlockSpec((1, span, lanes), lambda g, p, s: (g, p, 0)),
                 fixed(beams.shape),
                 fixed(taps.shape),
             ],
             out_specs=[
-                pl.BlockSpec((per, 2, rows, inputs), lambda g, p, s: (g * split + p, 0, 0, 0)),
+                pl.BlockSpec((QUAD, 2, rows, span), lambda g, p, s: (g, 0, 0, p)),
                 fixed((count, 2, frames_n * NCH)),
             ],
             scratch_shapes=[
-                pltpu.VMEM((rows, lanes), jnp.bfloat16),
-                pltpu.VMEM(((spectra_n + 2 * TAPS) * count, 2 * NCH), jnp.bfloat16),
+                pltpu.VMEM((2 * QUAD * rows, lanes), jnp.bfloat16),
+                pltpu.VMEM(((frames_n + VOICES + TAPS) * count, 2 * NCH), jnp.bfloat16),
                 pltpu.VMEM((TAPS, 2 * NCH, 2 * NCH), jnp.bfloat16),
             ],
         ),
@@ -704,20 +732,13 @@
     most = min(section, max(2, 2 * section // n_chan))
     fits = inp_dev == 64 and most == 32 and section == 64 and NCH == 128
     fits = fits and n_sub % 2 == 0 and ch_dev % (2 * QUAD) == 0 and inputs % 512 == 0
-    if not fits or 4 * ch_dev * QUAD < 11 + 2 * QUAD or rows % 128:
+    if not fits or n_sub != 4 or n_chan % 2 or n_chan > 8 or rows % 128:
         return local_plain(voltages, taps, input_id, counts, delays, beam_owner)
     sub_index = lax.axis_index("sub")
-    frames = voltages.reshape(inp_dev, 2, spectra_n + TAPS - 1, NCH)
-    frames = jnp.transpose(frames, (1, 2, 0, 3))
-    swapped = input_id.reshape(-1, 2, inp_dev)[:, ::-1].reshape(inputs)
-    names = jnp.stack([input_id, swapped])
-    owner = lax.dynamic_slice_in_dim(beam_owner[:, 0], sub_index * section, section)
-    beam = jnp.arange(section, dtype=jnp.int32)
-    earlier = (owner[None, :] == owner[:, None]) & (beam[None, :] < beam[:, None])
-    rank = jnp.sum(earlier.astype(jnp.int32), axis=1)
-    slots = (owner * (4 * most) + rank)[:, None]
+    owner = lax.dynamic_slice_in_dim(beam_owner[:, 0], sub_index * section, section)[None]
     taps2 = taps.reshape(TAPS, NCH)
-    by_id, beams = front(frames, taps2, counts, names, delays, slots, n_chan, n_sub, most)
+    names = input_id[None]
+    by_id, beams = front(voltages, taps2, counts, names, delays, owner, n_chan, n_sub, most)
     visibility, resynth = back(
         by_id, beams, taps2, counts, sub_index.astype(jnp.int32)[None], rows, most
     )

time: 94.2 us -> 95.5 us (1.014)
  Pallas kernels: 83.5 us -> 93.1 us
  local copies, waits for them, and re-layouts: 7.21 us -> 1.25 us
  other arithmetic: 2.09 us -> 0 us
    pallas_call x1, Pallas kernels: 57.5 us -> 68.1 us  [front(): pl.pallas_call(functools.partial(front_kernel, n_chan, n_sub, most), in_s...]
    reshape x3 -> x0, local copies, waits for them, and re-layouts: 6.08 us -> none  [the longest x2 5.31 us: local(): frames = voltages.reshape(inp_dev, 2, spectra_n + TAPS - 1, NCH)]
    another operation x1 -> x0, other arithmetic: 1.29 us -> none  [local(): names = jnp.stack([input_id, swapped])]
    pallas_call x1, Pallas kernels: 26 us -> 25 us  [back(): pl.pallas_call(back_kernel, grid_spec=pltpu.PrefetchScalarGridSpec(num_sc...]
where the time goes in v2:
time: 95.5 us; the launch traced here: 95 us
  Pallas kernels  93.1 us (97%)
  local copies, waits for them, and re-layouts  1.25 us (1%)
    pallas_call x1, Pallas kernels, front(): pl.pallas_call(functools.partial(front_kernel, n_chan, n_sub, most), in_s...  68.1 us
    pallas_call x1, Pallas kernels, back(): pl.pallas_call(back_kernel, grid_spec=pltpu.PrefetchScalarGridSpec(num_sc...  25 us

profile of v2, /device:TPU:0, one launch (start us, length us, event | category | flops | bytes accessed | tf_op | source)
XLA Modules:
  0.0 95.0 jit_solution(17189973338257669995)
XLA Ops:
  0.6 0.0 copy-start
  0.6 0.7 copy-done
  1.3 0.6 dynamic-slice_bitcast_fusion.owner_ref
  1.9 68.1 %front.1 = (bf16[8,1024,256]{2,1,0:T(8,128)(2,1)}, bf16[4,4,2,64,128]{4,3,2,1,0:T(8,128)(2,1)}) custom-call(bf16[64,2,5504]{2,1,0:T(2,128)(2,1)} %volt_ref.1, f32[12,128]{1,0:T(8,128)} %bitcast.7, s32[4]{0:T(128)} %counts_ref.3, s32[1,1024]{1,0:T(1,128)} %bitcast.9, s32[64,1024]{1,0:T(8,128)} %delay_ref.1, s32[1,64]{1,0:T(1,128)} %dynamic-slice_bitcast_fusion.owner_ref), custom_call_target="tpu_custom_call" | custom-call | tf_op jit(solution)/shard_map/front/pallas_call | solution.py:540
  70.0 25.0 %back.1 = (bf16[32,2,256,1024]{3,2,1,0:T(8,128)(2,1)}, f32[32,2,5504]{2,1,0:T(2,128)}) custom-call(s32[1]{0:T(128)} %bitcast.sub_ref, s32[4]{0:T(128)} %counts_ref.3, bf16[8,1024,256]{2,1,0:T(8,128)(2,1)} %get-tuple-element.4.mine_ref.all_ref, bf16[8,1024,256]{2,1,0:T(8,128)(2,1)} %get-tuple-element.4.mine_ref.all_ref, bf16[4,8,64,128]{3,2,1,0:T(8,128)(2,1)} %bitcast.6, ...), custom_call_target="tpu_custom_call" | custom-call | tf_op jit(solution)/shard_map/back/pallas_call | solution.py:692
Async XLA Ops:
  0.6 0.7 copy-start

commit v3 on v2

--- a/solution.py
+++ b/solution.py
@@ -175,7 +175,7 @@
     n_chan, n_sub, most,
     volt_ref, taps_ref, counts_ref, name_ref, delay_ref, owner_ref,
     sorted_ref, beams_ref,
-    v_ref, late_ref, x_ref, g_ref, y_ref, d_ref, perm_ref, turn_ref, c_ref, held, weight_ref,
+    v_ref, wide_ref, x_ref, g_ref, y_ref, d_ref, perm_ref, turn_ref, c_ref, held, weight_ref,
     place_ref, ready,
     load_sem, own_sem, out_sem, keep_sem, zs, zr, xs, xr, cs, cr, es, er,
 ):
@@ -270,17 +270,18 @@
     step = 16
     run = 4
     pltpu.make_async_copy(v_ref, v_ref, load_sem).wait()
-
-    @pl.loop(0, rows // step)
-    def _(it):
-        at = pl.multiple_of(it * step, step)
-        taps = [taps_ref[k : k + 1, :] for k in range(TAPS)]
-        for h in range(2):
+    for s in range(frames_n):
+        wide_ref[s] = v_ref[s].reshape(2 * rows, NCH).astype(jnp.float32)
+
+    for c in range(2):
+
+        @pl.loop(0, rows // step)
+        def _(it):
+            at = pl.multiple_of(it * step, step)
+            taps = [taps_ref[k : k + 1, :] for k in range(TAPS)]
             for first in range(0, spectra_n, run):
                 window = [
-                    v_ref[s, pl.ds(at + h * (step // 2), step // 2)]
-                    .reshape(step, NCH)
-                    .astype(jnp.float32)
+                    wide_ref[s, pl.ds(2 * at + c, step, stride=2), :]
                     for s in range(first, first + run + TAPS - 1)
                 ]
                 for j in range(run):
@@ -288,16 +289,13 @@
                     total = window[j] * taps[0]
                     for k in range(1, TAPS):
                         total = total + window[j + k] * taps[k]
-                    late_ref[t, h * step : (h + 1) * step, :] = total * valid[t]
-        for t in range(spectra_n):
-            slot = t // 2 * 2 + (t % 2 + core) % 2
-            to = pl.multiple_of(slot * rows + at, step)
-            for c in range(2):
-                total = late_ref[t, pl.ds(c, step, stride=2), :]
-                high = total.astype(jnp.bfloat16)
-                low = (total - high.astype(jnp.float32)).astype(jnp.bfloat16)
-                y_ref[pl.ds(to, step), c * NCH : (c + 1) * NCH] = high
-                y_ref[pl.ds(to, step), wide + c * NCH : wide + (c + 1) * NCH] = low
+                    total = total * valid[t]
+                    high = total.astype(jnp.bfloat16)
+                    low = (total - high.astype(jnp.float32)).astype(jnp.bfloat16)
+                    slot = t // 2 * 2 + (t % 2 + core) % 2
+                    to = pl.multiple_of(slot * rows + at, step)
+                    y_ref[pl.ds(to, step), c * NCH : (c + 1) * NCH] = high
+                    y_ref[pl.ds(to, step), wide + c * NCH : wide + (c + 1) * NCH] = low
 
     across_dims = (((1,), (1,)), ((), ()))
 
@@ -554,7 +552,7 @@
         ],
         scratch_shapes=[
             pltpu.VMEM((spectra_n + TAPS - 1, rows, 2, NCH), jnp.bfloat16),
-            pltpu.VMEM((spectra_n, 32, NCH), jnp.float32),
+            pltpu.VMEM((spectra_n + TAPS - 1, 2 * rows, NCH), jnp.float32),
             pltpu.VMEM((n_chan, pieces, per, block, 128), jnp.bfloat16),
             pltpu.VMEM((pieces, n_chan, n_sub, per, block, 128), jnp.bfloat16),
             pltpu.VMEM((spectra_n * rows, 4 * NCH), jnp.bfloat16),
@@ -585,14 +583,13 @@
 
 
 def back_kernel(
-    sub_ref, counts_ref, mine_ref, all_ref, beams_ref, taps_ref,
+    sub_ref, counts_ref, start_ref, mine_ref, all_ref, beams_ref, taps_ref,
     out_ref, voice_ref,
     left_ref, bank_ref, table_ref,
 ):
-    g, part = pl.program_id(0), pl.program_id(1)
-    step = g * pl.num_programs(1) + part
+    g = pl.program_id(0)
     rows, lanes = mine_ref.shape[1], mine_ref.shape[2]
-    span = all_ref.shape[1]
+    inputs = all_ref.shape[1]
     count, _, samples = voice_ref.shape
     frames_n = samples // NCH
     spectra_n = frames_n - TAPS + 1
@@ -604,22 +601,26 @@
     scale = 1.0 / jnp.full((8, 128), total.astype(jnp.float32))
     scale = scale[:1, :1]
 
-    @pl.when(part == 0)
+    def fill(ref, slot, lanes_kept):
+        plain = ref[0]
+        real, after, before = partner(plain.astype(jnp.float32), lanes)
+        turned = jnp.where(real, after, -before).astype(jnp.bfloat16)
+        lane = lax.broadcasted_iota(jnp.int32, (16, lanes), 1) % QUAD
+        for i in lanes_kept:
+            keep = jnp.where(lane == i, 1.0, 0.0).astype(jnp.bfloat16)
+            keep = jnp.concatenate([keep] * (rows // 16), axis=0)
+            at = pl.multiple_of(2 * i * rows, rows)
+            left_ref[slot, pl.ds(at, rows), :] = plain * keep
+            left_ref[slot, pl.ds(at + rows, rows), :] = turned * keep
+
+    @pl.when(g == 0)
     def _():
-        plain = mine_ref[0].astype(jnp.float32)
-        real, after, before = partner(plain, lanes)
-        turned = jnp.where(real, after, -before)
-        lane = lax.broadcasted_iota(jnp.int32, (rows, lanes), 1) % QUAD
-        for i in range(QUAD):
-            at = 2 * i * rows
-            left_ref[at : at + rows, :] = jnp.where(lane == i, plain, 0.0).astype(jnp.bfloat16)
-            left_ref[at + rows : at + 2 * rows, :] = jnp.where(lane == i, turned, 0.0).astype(
-                jnp.bfloat16
-            )
-
-    for at in range(0, span, 256):
+        fill(start_ref, 0, range(QUAD))
+
+    fill(mine_ref, (g + 1) % 2, range(QUAD))
+    for at in range(0, inputs, 256):
         product = lax.dot_general(
-            left_ref[...],
+            left_ref[g % 2],
             all_ref[0, at : at + 256, :],
             (((1,), (1,)), ((), ())),
             preferred_element_type=jnp.float32,
@@ -630,7 +631,7 @@
                 low = (2 * i + c) * rows
                 out_ref[i, c, :, at : at + 256] = product[low : low + rows]
 
-    @pl.when(step == 0)
+    @pl.when(g == 0)
     def _():
         edge = (TAPS - 1) * count
         bank_ref[:edge, :] = jnp.zeros((edge, 2 * NCH), jnp.bfloat16)
@@ -647,7 +648,7 @@
                 at = edge + (u + v) * 4 * count
                 bank_ref[at : at + 4 * count, :] = stack.T.astype(jnp.bfloat16)
 
-    @pl.when(step == 1)
+    @pl.when(g == 0)
     def _():
         trig = trig_of((2 * NCH, 2 * NCH), n_grp)
         for k in range(TAPS):
@@ -655,7 +656,7 @@
             table_ref[k] = (trig * jnp.concatenate([taps, taps], axis=1)).astype(jnp.bfloat16)
 
     run = VOICES
-    chunk = step - 2
+    chunk = g - 1
 
     @pl.when((chunk >= 0) & (chunk * run < frames_n))
     def _():
@@ -684,29 +685,34 @@
     beams = beams.reshape((n_chan, n_grp) + beams.shape[3:])
     spectra_n = BLOCKS * SPEC
     frames_n = spectra_n + TAPS - 1
-    split = 2
-    span = inputs // split
     fixed = lambda shape: pl.BlockSpec(
-        shape, lambda g, p, s: (0,) * len(shape), pipeline_mode=pl.Buffered(1)
+        shape, lambda g, s: (0,) * len(shape), pipeline_mode=pl.Buffered(1)
     )
     return pl.pallas_call(
         back_kernel,
         grid_spec=pltpu.PrefetchScalarGridSpec(
             num_scalar_prefetch=1,
-            grid=(n_grp, split),
+            grid=(n_grp,),
             in_specs=[
                 pl.BlockSpec(memory_space=pltpu.SMEM),
-                pl.BlockSpec((1, rows, lanes), lambda g, p, s: (g, s[0], 0)),
-                pl.BlockSpec((1, span, lanes), lambda g, p, s: (g, p, 0)),
+                pl.BlockSpec(
+                    (1, rows, lanes),
+                    lambda g, s: (0, s[0], 0),
+                    pipeline_mode=pl.Buffered(1),
+                ),
+                pl.BlockSpec(
+                    (1, rows, lanes), lambda g, s: (jnp.minimum(g + 1, n_grp - 1), s[0], 0)
+                ),
+                pl.BlockSpec((1, inputs, lanes), lambda g, s: (g, 0, 0)),
                 fixed(beams.shape),
                 fixed(taps.shape),
             ],
             out_specs=[
-                pl.BlockSpec((QUAD, 2, rows, span), lambda g, p, s: (g, 0, 0, p)),
+                pl.BlockSpec((QUAD, 2, rows, inputs), lambda g, s: (g, 0, 0, 0)),
                 fixed((count, 2, frames_n * NCH)),
             ],
             scratch_shapes=[
-                pltpu.VMEM((2 * QUAD * rows, lanes), jnp.bfloat16),
+                pltpu.VMEM((2, 2 * QUAD * rows, lanes), jnp.bfloat16),
                 pltpu.VMEM(((frames_n + VOICES + TAPS) * count, 2 * NCH), jnp.bfloat16),
                 pltpu.VMEM((TAPS, 2 * NCH, 2 * NCH), jnp.bfloat16),
             ],
@@ -715,9 +721,9 @@
             jax.ShapeDtypeStruct((n_grp * QUAD, 2, rows, inputs), jnp.bfloat16),
             jax.ShapeDtypeStruct((count, 2, frames_n * NCH), jnp.float32),
         ],
-        compiler_params=pltpu.CompilerParams(dimension_semantics=("arbitrary", "arbitrary")),
+        compiler_params=pltpu.CompilerParams(dimension_semantics=("arbitrary",)),
         name="back",
-    )(sub_index, counts, by_id, by_id, beams, taps)
+    )(sub_index, counts, by_id, by_id, by_id, beams, taps)
 
 
 def local(voltages, taps, input_id, counts, delays, beam_owner):

time: 95.5 us -> 82.9 us (0.87)
  Pallas kernels: 93.1 us -> 80.7 us
    pallas_call x1, Pallas kernels: 68.1 us -> 59.8 us  [front(): pl.pallas_call(functools.partial(front_kernel, n_chan, n_sub, most), in_s...]
    pallas_call x1, Pallas kernels: 25 us -> 20.8 us  [back(): pl.pallas_call(back_kernel, grid_spec=pltpu.PrefetchScalarGridSpec(num_sc...]
where the time goes in v3:
time: 82.9 us; the launch traced here: 82.6 us
  Pallas kernels  80.7 us (97%)
  local copies, waits for them, and re-layouts  1.25 us (2%)
    pallas_call x1, Pallas kernels, front(): pl.pallas_call(functools.partial(front_kernel, n_chan, n_sub, most), in_s...  59.8 us
    pallas_call x1, Pallas kernels, back(): pl.pallas_call(back_kernel, grid_spec=pltpu.PrefetchScalarGridSpec(num_sc...  20.8 us

profile of v3, /device:TPU:0, one launch (start us, length us, event | category | flops | bytes accessed | tf_op | source)
XLA Modules:
  0.0 82.6 jit_solution(7658102876336045280)
XLA Ops:
  0.6 0.0 copy-start
  0.6 0.7 copy-done
  1.3 0.6 dynamic-slice_bitcast_fusion.owner_ref
  1.9 59.8 %front.1 = (bf16[8,1024,256]{2,1,0:T(8,128)(2,1)}, bf16[4,4,2,64,128]{4,3,2,1,0:T(8,128)(2,1)}) custom-call(bf16[64,2,5504]{2,1,0:T(2,128)(2,1)} %volt_ref.1, f32[12,128]{1,0:T(8,128)} %bitcast.7, s32[4]{0:T(128)} %counts_ref.3, s32[1,1024]{1,0:T(1,128)} %bitcast.9, s32[64,1024]{1,0:T(8,128)} %delay_ref.1, s32[1,64]{1,0:T(1,128)} %dynamic-slice_bitcast_fusion.owner_ref), custom_call_target="tpu_custom_call" | custom-call | tf_op jit(solution)/shard_map/front/pallas_call | solution.py:538
  61.7 20.8 %back.1 = (bf16[32,2,256,1024]{3,2,1,0:T(8,128)(2,1)}, f32[32,2,5504]{2,1,0:T(2,128)}) custom-call(s32[1]{0:T(128)} %bitcast.sub_ref, s32[4]{0:T(128)} %counts_ref.3, bf16[8,1024,256]{2,1,0:T(8,128)(2,1)} %get-tuple-element.4.start_ref.mine_ref.all_ref, bf16[8,1024,256]{2,1,0:T(8,128)(2,1)} %get-tuple-element.4.start_ref.mine_ref.all_ref, ...), custom_call_target="tpu_custom_call" | custom-call | tf_op jit(solution)/shard_map/back/pallas_call | solution.py:691
Async XLA Ops:
  0.6 0.7 copy-start

commit v4 on v3

--- a/solution.py
+++ b/solution.py
@@ -149,7 +149,7 @@
 
 
 QUAD = 4
-VOICES = 8
+VOICES = 4
 
 
 def trig_of(shape, n_grp):
@@ -195,8 +195,14 @@
     wide = 2 * NCH
     block = x_ref.shape[3]
 
-    def chan_of(offset):
-        return (me_c + offset) % n_chan
+    def chan_of(k):
+        at = me_c
+        bit = 1
+        while bit < n_chan:
+            if k & bit:
+                at = at + bit - 2 * bit * (me_c // bit % 2)
+            bit *= 2
+        return at
 
     def sub_of(offset):
         return (across + offset) % n_x * 2 + core
@@ -226,12 +232,12 @@
     def source(j, q):
         if j == 0:
             return x_ref.at[me_c, q]
-        return g_ref.at[q, chan_of(n_chan - j), me_s]
+        return g_ref.at[q, chan_of(j), me_s]
 
     def x_copy(dx, j, q):
         return pltpu.make_async_remote_copy(
             src_ref=source(j, q),
-            dst_ref=g_ref.at[q, chan_of(n_chan - j), me_s],
+            dst_ref=g_ref.at[q, chan_of(j), me_s],
             send_sem=xs,
             recv_sem=xr.at[dx - 1, j, q],
             device_id={"sub": sub_of(dx)},
@@ -239,7 +245,7 @@
         )
 
     def core_copy(dx, j, q):
-        home = g_ref.at[q, chan_of(n_chan - j), sub_of(n_x - dx)]
+        home = g_ref.at[q, chan_of(j), sub_of(n_x - dx)]
         return pltpu.make_async_remote_copy(
             src_ref=source(j, q) if dx == 0 else home,
             dst_ref=home,
@@ -502,13 +508,27 @@
         weigh_unit(at, left) for at in range(0, beams_n, 16) for left in range(0, inputs, 512)
     ]
     setup.append(place_unit)
-    weave(setup, [z_step(j, 0) for j in range(1, n_chan)])
+    def z_steps(q):
+        return [z_step(j, q) for j in range(1, n_chan)] if q < pieces else []
+
+    def x_steps(q):
+        return [functools.partial(x_step, j, q) for j in range(n_chan)]
+
+    def mingle(one, two):
+        pairs = [(i / len(one), 0, s) for i, s in enumerate(one)]
+        pairs += [((i + 0.5) / len(two), 1, s) for i, s in enumerate(two)]
+        return [s for _, _, s in sorted(pairs, key=lambda p: p[:2])]
+
+    weave(setup[:7], z_steps(0))
     for q in range(1, pieces + 1):
-        for j in range(n_chan):
-            x_step(j, q - 1)
-        arrive(q - 1)
-        steps = [z_step(j, q) for j in range(1, n_chan)] if q < pieces else []
-        weave(units_of(q - 1), steps)
+        steps = mingle(x_steps(q - 1), z_steps(q))
+        if q >= 2:
+            arrive(q - 2)
+            weave(units_of(q - 2), steps)
+        else:
+            weave(setup[7:], steps)
+    arrive(pieces - 1)
+    weave(units_of(pieces - 1), [])
     others = pl.ds(0, n_chan - 1)
     pltpu.make_async_copy(ready.at[others], beams_ref.at[others], er).wait()
     pltpu.make_async_copy(x_ref.at[others], x_ref.at[others], zs).wait()
@@ -583,60 +603,71 @@
 
 
 def back_kernel(
-    sub_ref, counts_ref, start_ref, mine_ref, all_ref, beams_ref, taps_ref,
-    out_ref, voice_ref,
-    left_ref, bank_ref, table_ref,
+    sub_ref, counts_ref, sorted_ref, heard_ref, taps_ref,
+    out_ref, voices_ref,
+    all_ref, beams_ref, left_ref, bank_ref, wave_ref, made_ref, mix_ref, voice_ref,
+    in_sem, heard_sem, out_sem, voice_sem,
 ):
-    g = pl.program_id(0)
-    rows, lanes = mine_ref.shape[1], mine_ref.shape[2]
-    inputs = all_ref.shape[1]
-    count, _, samples = voice_ref.shape
-    frames_n = samples // NCH
+    n_grp, inputs, lanes = all_ref.shape
+    rows, wide = made_ref.shape[4:]
+    frames_n, count = voice_ref.shape[:2]
     spectra_n = frames_n - TAPS + 1
-    n_chan, n_grp = beams_ref.shape[0], beams_ref.shape[1]
+    n_chan = beams_ref.shape[0]
     tile = 2 * QUAD
+    mine = pl.ds(pl.multiple_of(sub_ref[0] * rows, rows), rows)
+
+    def in_copy(g):
+        return pltpu.make_async_copy(sorted_ref.at[g], all_ref.at[g], in_sem.at[g])
+
+    def out_copy(g, n):
+        return pltpu.make_async_copy(
+            made_ref.at[g % 2, n],
+            out_ref.at[pl.ds(g * QUAD, QUAD), :, :, pl.ds(n * wide, wide)],
+            out_sem.at[g % 2, n],
+        )
+
+    heard = pltpu.make_async_copy(heard_ref, beams_ref, heard_sem)
+    for g in range(n_grp):
+        in_copy(g).start()
+        if g == 0:
+            heard.start()
     total = counts_ref[0]
     for i in range(1, BLOCKS):
         total = total + counts_ref[i]
     scale = 1.0 / jnp.full((8, 128), total.astype(jnp.float32))
     scale = scale[:1, :1]
-
-    def fill(ref, slot, lanes_kept):
-        plain = ref[0]
+    lane = lax.broadcasted_iota(jnp.int32, (16, lanes), 1) % QUAD
+    keeps = []
+    for i in range(QUAD):
+        keep = jnp.where(lane == i, 1.0, 0.0).astype(jnp.bfloat16)
+        keeps.append(jnp.concatenate([keep] * (rows // 16), axis=0))
+
+    def fill(g):
+        plain = all_ref[g, mine, :]
         real, after, before = partner(plain.astype(jnp.float32), lanes)
         turned = jnp.where(real, after, -before).astype(jnp.bfloat16)
-        lane = lax.broadcasted_iota(jnp.int32, (16, lanes), 1) % QUAD
-        for i in lanes_kept:
-            keep = jnp.where(lane == i, 1.0, 0.0).astype(jnp.bfloat16)
-            keep = jnp.concatenate([keep] * (rows // 16), axis=0)
-            at = pl.multiple_of(2 * i * rows, rows)
-            left_ref[slot, pl.ds(at, rows), :] = plain * keep
-            left_ref[slot, pl.ds(at + rows, rows), :] = turned * keep
-
-    @pl.when(g == 0)
-    def _():
-        fill(start_ref, 0, range(QUAD))
-
-    fill(mine_ref, (g + 1) % 2, range(QUAD))
-    for at in range(0, inputs, 256):
-        product = lax.dot_general(
-            left_ref[g % 2],
-            all_ref[0, at : at + 256, :],
-            (((1,), (1,)), ((), ())),
-            preferred_element_type=jnp.float32,
-        )
-        product = (product * scale).astype(jnp.bfloat16)
         for i in range(QUAD):
-            for c in range(2):
-                low = (2 * i + c) * rows
-                out_ref[i, c, :, at : at + 256] = product[low : low + rows]
-
-    @pl.when(g == 0)
-    def _():
-        edge = (TAPS - 1) * count
-        bank_ref[:edge, :] = jnp.zeros((edge, 2 * NCH), jnp.bfloat16)
-        end = edge + spectra_n * count
-        bank_ref[end:, :] = jnp.zeros((bank_ref.shape[0] - end, 2 * NCH), jnp.bfloat16)
+            at = 2 * i * rows
+            left_ref[g % 2, at : at + rows, :] = plain * keeps[i]
+            left_ref[g % 2, at + rows : at + 2 * rows, :] = turned * keeps[i]
+
+    def correlate(g):
+        for n in range(inputs // wide):
+            product = lax.dot_general(
+                left_ref[g % 2],
+                all_ref[g, n * wide : (n + 1) * wide, :],
+                (((1,), (1,)), ((), ())),
+                preferred_element_type=jnp.float32,
+            )
+            product = (product * scale).astype(jnp.bfloat16)
+            for i in range(QUAD):
+                for c in range(2):
+                    low = (2 * i + c) * rows
+                    made_ref[g % 2, n, i, c] = product[low : low + rows]
+            out_copy(g, n).start()
+
+    def line_up():
+        heard.wait()
         for u in range(0, spectra_n // 4, 2):
             tiles = [
                 beams_ref[c, e, u * tile : (u + 2) * tile, :].astype(jnp.float32)
@@ -645,38 +676,67 @@
             ]
             for v in range(2):
                 stack = jnp.concatenate([t[v * tile : (v + 1) * tile] for t in tiles], axis=0)
-                at = edge + (u + v) * 4 * count
+                at = (u + v) * 4 * count
                 bank_ref[at : at + 4 * count, :] = stack.T.astype(jnp.bfloat16)
 
-    @pl.when(g == 0)
-    def _():
+    def transform():
         trig = trig_of((2 * NCH, 2 * NCH), n_grp)
-        for k in range(TAPS):
-            taps = taps_ref[k : k + 1, :]
-            table_ref[k] = (trig * jnp.concatenate([taps, taps], axis=1)).astype(jnp.bfloat16)
-
-    run = VOICES
-    chunk = g - 1
-
-    @pl.when((chunk >= 0) & (chunk * run < frames_n))
-    def _():
-        acc = jnp.zeros((run * count, 2 * NCH), jnp.float32)
-        for k in range(TAPS):
-            start = pl.multiple_of((chunk * run - k + TAPS - 1) * count, count)
-            acc = acc + jnp.dot(
-                bank_ref[pl.ds(start, run * count), :],
-                table_ref[k],
-                preferred_element_type=jnp.float32,
-            )
+        high = trig.astype(jnp.bfloat16)
+        low = (trig - high.astype(jnp.float32)).astype(jnp.bfloat16)
+        wave_ref[...] = jnp.dot(
+            bank_ref[...], high, preferred_element_type=jnp.float32
+        ) + jnp.dot(bank_ref[...], low, preferred_element_type=jnp.float32)
+
+    def speak(first):
+        run = min(VOICES, frames_n - first)
+        for c in range(2):
+            lanes = slice(c * NCH, (c + 1) * NCH)
+            taps = [taps_ref[k : k + 1, :] for k in range(TAPS)]
+            for p in range(0, count, 8):
+                window = {
+                    s: wave_ref[s * count + p : s * count + p + 8, lanes]
+                    for s in range(max(0, first - TAPS + 1), min(spectra_n, first + run))
+                }
+                for j in range(run):
+                    terms = [
+                        window[first + j - k] * taps[k]
+                        for k in range(TAPS)
+                        if 0 <= first + j - k < spectra_n
+                    ]
+                    total = terms[0]
+                    for term in terms[1:]:
+                        total = total + term
+                    mix_ref[first + j, pl.ds(2 * p + c, 8, stride=2), :] = total
         for j in range(run):
-
-            @pl.when(chunk * run + j < frames_n)
-            def _():
-                at = pl.multiple_of((chunk * run + j) * NCH, NCH)
-                for c in range(2):
-                    voice_ref[:, c, pl.ds(at, NCH)] = acc[
-                        j * count : (j + 1) * count, c * NCH : (c + 1) * NCH
-                    ]
+            voice_ref[first + j] = mix_ref[first + j].reshape(count, 2, NCH)
+            pltpu.make_async_copy(
+                voice_ref.at[first + j],
+                voices_ref.at[:, :, pl.ds((first + j) * NCH, NCH)],
+                voice_sem,
+            ).start()
+
+    jobs = [line_up, transform]
+    jobs += [functools.partial(speak, first) for first in range(0, frames_n, VOICES)]
+    shares = n_grp - 1
+    done = 0
+    in_copy(0).wait()
+    fill(0)
+    for g in range(n_grp):
+        if g >= 2:
+            for n in range(inputs // wide):
+                out_copy(g - 2, n).wait()
+        if g + 1 < n_grp:
+            in_copy(g + 1).wait()
+            fill(g + 1)
+        correlate(g)
+        upto = min(len(jobs), -(-len(jobs) * (g + 1) // shares))
+        for job in jobs[done:upto]:
+            job()
+        done = upto
+    for g in range(n_grp - 2, n_grp):
+        for n in range(inputs // wide):
+            out_copy(g, n).wait()
+    pltpu.make_async_copy(voice_ref, voice_ref, voice_sem).wait()
 
 
 def back(by_id, beams, taps, counts, sub_index, rows, count):
@@ -685,45 +745,33 @@
     beams = beams.reshape((n_chan, n_grp) + beams.shape[3:])
     spectra_n = BLOCKS * SPEC
     frames_n = spectra_n + TAPS - 1
-    fixed = lambda shape: pl.BlockSpec(
-        shape, lambda g, s: (0,) * len(shape), pipeline_mode=pl.Buffered(1)
-    )
+    wide = 512
+    hbm = pl.BlockSpec(memory_space=pl.ANY)
+    smem = pl.BlockSpec(memory_space=pltpu.SMEM)
     return pl.pallas_call(
         back_kernel,
-        grid_spec=pltpu.PrefetchScalarGridSpec(
-            num_scalar_prefetch=1,
-            grid=(n_grp,),
-            in_specs=[
-                pl.BlockSpec(memory_space=pltpu.SMEM),
-                pl.BlockSpec(
-                    (1, rows, lanes),
-                    lambda g, s: (0, s[0], 0),
-                    pipeline_mode=pl.Buffered(1),
-                ),
-                pl.BlockSpec(
-                    (1, rows, lanes), lambda g, s: (jnp.minimum(g + 1, n_grp - 1), s[0], 0)
-                ),
-                pl.BlockSpec((1, inputs, lanes), lambda g, s: (g, 0, 0)),
-                fixed(beams.shape),
-                fixed(taps.shape),
-            ],
-            out_specs=[
-                pl.BlockSpec((QUAD, 2, rows, inputs), lambda g, s: (g, 0, 0, 0)),
-                fixed((count, 2, frames_n * NCH)),
-            ],
-            scratch_shapes=[
-                pltpu.VMEM((2, 2 * QUAD * rows, lanes), jnp.bfloat16),
-                pltpu.VMEM(((frames_n + VOICES + TAPS) * count, 2 * NCH), jnp.bfloat16),
-                pltpu.VMEM((TAPS, 2 * NCH, 2 * NCH), jnp.bfloat16),
-            ],
-        ),
+        in_specs=[smem, smem, hbm, hbm, pl.BlockSpec(memory_space=pltpu.VMEM)],
+        out_specs=[hbm, hbm],
+        scratch_shapes=[
+            pltpu.VMEM(by_id.shape, jnp.bfloat16),
+            pltpu.VMEM(beams.shape, jnp.bfloat16),
+            pltpu.VMEM((2, 2 * QUAD * rows, lanes), jnp.bfloat16),
+            pltpu.VMEM((spectra_n * count, 2 * NCH), jnp.bfloat16),
+            pltpu.VMEM((spectra_n * count, 2 * NCH), jnp.float32),
+            pltpu.VMEM((2, inputs // wide, QUAD, 2, rows, wide), jnp.bfloat16),
+            pltpu.VMEM((frames_n, 2 * count, NCH), jnp.float32),
+            pltpu.VMEM((frames_n, count, 2, NCH), jnp.float32),
+            pltpu.SemaphoreType.DMA((n_grp,)),
+            pltpu.SemaphoreType.DMA,
+            pltpu.SemaphoreType.DMA((2, inputs // wide)),
+            pltpu.SemaphoreType.DMA,
+        ],
         out_shape=[
             jax.ShapeDtypeStruct((n_grp * QUAD, 2, rows, inputs), jnp.bfloat16),
             jax.ShapeDtypeStruct((count, 2, frames_n * NCH), jnp.float32),
         ],
-        compiler_params=pltpu.CompilerParams(dimension_semantics=("arbitrary",)),
         name="back",
-    )(sub_index, counts, by_id, by_id, by_id, beams, taps)
+    )(sub_index, counts, by_id, beams, taps)
 
 
 def local(voltages, taps, input_id, counts, delays, beam_owner):

time: 82.9 us -> 70.1 us (0.85)
  Pallas kernels: 80.7 us -> 67.7 us
    pallas_call x1, Pallas kernels: 59.8 us -> 51 us  [front(): pl.pallas_call(functools.partial(front_kernel, n_chan, n_sub, most), in_s...]
    pallas_call x1, Pallas kernels: 20.8 us -> 16.8 us  [back(): pl.pallas_call(back_kernel, in_specs=[smem, smem, hbm, hbm, pl.BlockSpec(...]
where the time goes in v4:
time: 70.1 us; the launch traced here: 69.8 us
  Pallas kernels  67.7 us (97%)
  local copies, waits for them, and re-layouts  1.25 us (2%)
  between operations  0.83 us (1%)
    pallas_call x1, Pallas kernels, front(): pl.pallas_call(functools.partial(front_kernel, n_chan, n_sub, most), in_s...  51 us
    pallas_call x1, Pallas kernels, back(): pl.pallas_call(back_kernel, in_specs=[smem, smem, hbm, hbm, pl.BlockSpec(...  16.8 us

profile of v4, /device:TPU:0, one launch (start us, length us, event | category | flops | bytes accessed | tf_op | source)
XLA Modules:
  0.0 69.8 jit_solution(7687772628322520258)
XLA Ops:
  0.6 0.0 copy-start
  0.6 0.7 copy-done
  1.3 0.6 dynamic-slice_bitcast_fusion.owner_ref
  1.9 51.0 %front.1 = (bf16[8,1024,256]{2,1,0:T(8,128)(2,1)}, bf16[4,4,2,64,128]{4,3,2,1,0:T(8,128)(2,1)}) custom-call(bf16[64,2,5504]{2,1,0:T(2,128)(2,1)} %volt_ref.1, f32[12,128]{1,0:T(8,128)} %bitcast.7, s32[4]{0:T(128)} %counts_ref.3, s32[1,1024]{1,0:T(1,128)} %bitcast.9, s32[64,1024]{1,0:T(8,128)} %delay_ref.1, s32[1,64]{1,0:T(1,128)} %dynamic-slice_bitcast_fusion.owner_ref), custom_call_target="tpu_custom_call" | custom-call | tf_op jit(solution)/shard_map/front/pallas_call | solution.py:558
  52.9 16.8 %back.1 = (bf16[32,2,256,1024]{3,2,1,0:T(8,128)(2,1)}, f32[32,2,5504]{2,1,0:T(2,128)}) custom-call(s32[1]{0:T(128)} %bitcast.sub_ref, s32[4]{0:T(128)} %counts_ref.3, bf16[8,1024,256]{2,1,0:T(8,128)(2,1)} %get-tuple-element.4.sorted_ref, bf16[4,8,64,128]{3,2,1,0:T(8,128)(2,1)} %bitcast.6, f32[12,128]{1,0:T(8,128)} %bitcast.8), custom_call_target="tpu_custom_call" | custom-call | tf_op jit(solution)/shard_map/back/pallas_call | solution.py:751
Async XLA Ops:
  0.6 0.7 copy-start

commit v5 on v4

--- a/solution.py
+++ b/solution.py
@@ -305,7 +305,7 @@
 
     across_dims = (((1,), (1,)), ((), ()))
 
-    @pl.loop(0, spectra_n // 4)
+    @pl.loop(0, spectra_n // 4, unroll=2)
     def _(u):
         at = pl.multiple_of(u * 4 * rows, 4 * rows)
         high = y_ref[pl.ds(at, 4 * rows), :wide]
@@ -367,7 +367,12 @@
 
     def place_unit():
         lanes = per * beams_n
-        owner = jnp.concatenate([owner_ref[...]] * per, axis=1)
+        own = owner_ref[:, :beams_n] * (me_s == 0).astype(jnp.int32)
+        for s in range(1, n_sub):
+            own = own + owner_ref[:, s * beams_n : (s + 1) * beams_n] * (me_s == s).astype(
+                jnp.int32
+            )
+        owner = jnp.concatenate([own] * per, axis=1)
         named = (lax.broadcasted_iota(jnp.int32, (8, lanes), 0) == owner).astype(jnp.float32)
         row = lax.broadcasted_iota(jnp.int32, (lanes, lanes), 0)
         lane = lax.broadcasted_iota(jnp.int32, (lanes, lanes), 1)
@@ -456,7 +461,7 @@
                 for d in range(n_chan):
                     at = (e * n_chan + d) * 128
                     ready[d, q, e] = out[:, at : at + 128]
-            for j in range(1, n_chan):
+            for j in range(n_chan - 1, 0, -1):
                 beam_copy(j, q).start()
             pltpu.make_async_copy(ready.at[me_c, q], beams_ref.at[me_c, q], own_sem).start()
 
@@ -627,10 +632,9 @@
         )
 
     heard = pltpu.make_async_copy(heard_ref, beams_ref, heard_sem)
-    for g in range(n_grp):
-        in_copy(g).start()
-        if g == 0:
-            heard.start()
+    in_copy(0).start()
+    in_copy(1).start()
+    heard.start()
     total = counts_ref[0]
     for i in range(1, BLOCKS):
         total = total + counts_ref[i]
@@ -727,6 +731,8 @@
                 out_copy(g - 2, n).wait()
         if g + 1 < n_grp:
             in_copy(g + 1).wait()
+            if g + 2 < n_grp:
+                in_copy(g + 2).start()
             fill(g + 1)
         correlate(g)
         upto = min(len(jobs), -(-len(jobs) * (g + 1) // shares))
@@ -789,7 +795,7 @@
     if not fits or n_sub != 4 or n_chan % 2 or n_chan > 8 or rows % 128:
         return local_plain(voltages, taps, input_id, counts, delays, beam_owner)
     sub_index = lax.axis_index("sub")
-    owner = lax.dynamic_slice_in_dim(beam_owner[:, 0], sub_index * section, section)[None]
+    owner = beam_owner.reshape(1, -1)
     taps2 = taps.reshape(TAPS, NCH)
     names = input_id[None]
     by_id, beams = front(voltages, taps2, counts, names, delays, owner, n_chan, n_sub, most)

time: 70.1 us -> 68.3 us (0.974)
  local copies, waits for them, and re-layouts: 1.25 us -> 0 us
where the time goes in v5:
time: 68.3 us; the launch traced here: 68 us
  Pallas kernels  67.2 us (98%)
  between operations  0.82 us (1%)
    pallas_call x1, Pallas kernels, front(): pl.pallas_call(functools.partial(front_kernel, n_chan, n_sub, most), in_s...  50.4 us
    pallas_call x1, Pallas kernels, back(): pl.pallas_call(back_kernel, in_specs=[smem, smem, hbm, hbm, pl.BlockSpec(...  16.8 us

profile of v5, /device:TPU:0, one launch (start us, length us, event | category | flops | bytes accessed | tf_op | source)
XLA Modules:
  0.0 68.0 jit_solution(2947106091871151698)
XLA Ops:
  0.6 50.4 %front.1 = (bf16[8,1024,256]{2,1,0:T(8,128)(2,1)}, bf16[4,4,2,64,128]{4,3,2,1,0:T(8,128)(2,1)}) custom-call(bf16[64,2,5504]{2,1,0:T(2,128)(2,1)} %volt_ref.1, f32[12,128]{1,0:T(8,128)} %bitcast.6, s32[4]{0:T(128)} %counts_ref.3, s32[1,1024]{1,0:T(1,128)} %bitcast.8, s32[64,1024]{1,0:T(8,128)} %delay_ref.1, s32[1,256]{1,0:T(1,128)} %bitcast.9), custom_call_target="tpu_custom_call" | custom-call | tf_op jit(solution)/shard_map/front/pallas_call | solution.py:563
  51.1 16.8 %back.1 = (bf16[32,2,256,1024]{3,2,1,0:T(8,128)(2,1)}, f32[32,2,5504]{2,1,0:T(2,128)}) custom-call(s32[1]{0:T(128)} %bitcast.sub_ref, s32[4]{0:T(128)} %counts_ref.3, bf16[8,1024,256]{2,1,0:T(8,128)(2,1)} %get-tuple-element.4.sorted_ref, bf16[4,8,64,128]{3,2,1,0:T(8,128)(2,1)} %bitcast.5, f32[12,128]{1,0:T(8,128)} %bitcast.7), custom_call_target="tpu_custom_call" | custom-call | tf_op jit(solution)/shard_map/back/pallas_call | solution.py:757

commit v6 on v5

--- a/solution.py
+++ b/solution.py
@@ -401,10 +401,10 @@
                         a = g_ref[q, c, 2 * x, e].astype(jnp.float32)
                         b = g_ref[q, c, 2 * x + 1, e].astype(jnp.float32)
                         at = (c * n_x + x) * 128
-                        c_ref[low : low + block, at : at + 128] = jnp.where(left, a, b).astype(
+                        c_ref[q % 2, low : low + block, at : at + 128] = jnp.where(left, a, b).astype(
                             jnp.bfloat16
                         )
-                        c_ref[low + block : low + 2 * block, at : at + 128] = pltpu.roll(
+                        c_ref[q % 2, low + block : low + 2 * block, at : at + 128] = pltpu.roll(
                             jnp.where(left, b, a), 64, 1
                         ).astype(jnp.bfloat16)
 
@@ -414,7 +414,7 @@
         def run_unit():
             held[q * per + e, m * half : (m + 1) * half, :] = lax.dot_general(
                 perm_ref[m * half : (m + 1) * half, :],
-                c_ref[2 * e * block : 2 * (e + 1) * block, :],
+                c_ref[q % 2, 2 * e * block : 2 * (e + 1) * block, :],
                 across_dims,
                 preferred_element_type=jnp.float32,
             ).astype(jnp.bfloat16)
@@ -431,7 +431,7 @@
             for f in range(QUAD):
                 mixed = lax.dot_general(
                     weight_ref[at * QUAD + f],
-                    c_ref[2 * e * block : 2 * (e + 1) * block, :],
+                    c_ref[q % 2, 2 * e * block : 2 * (e + 1) * block, :],
                     across_dims,
                     preferred_element_type=jnp.float32,
                 )
@@ -474,9 +474,11 @@
 
         return run_unit
 
-    def units_of(q):
-        units = [join_unit(q)] + [mix_unit(q, e) for e in range(per)] + [place_beams(q)]
-        units += [sort_unit(q, e, m) for e in range(per) for m in range(4)]
+    def beams_of(q):
+        return [join_unit(q)] + [mix_unit(q, e) for e in range(per)] + [place_beams(q)]
+
+    def sorts_of(q):
+        units = [sort_unit(q, e, m) for e in range(per) for m in range(4)]
         return units + [store_unit(q)]
 
     def z_step(j, q):
@@ -529,11 +531,11 @@
         steps = mingle(x_steps(q - 1), z_steps(q))
         if q >= 2:
             arrive(q - 2)
-            weave(units_of(q - 2), steps)
+            weave(beams_of(q - 2) + (sorts_of(q - 2) if q < pieces else []), steps)
         else:
             weave(setup[7:], steps)
     arrive(pieces - 1)
-    weave(units_of(pieces - 1), [])
+    weave(beams_of(pieces - 1) + sorts_of(pieces - 2) + sorts_of(pieces - 1), [])
     others = pl.ds(0, n_chan - 1)
     pltpu.make_async_copy(ready.at[others], beams_ref.at[others], er).wait()
     pltpu.make_async_copy(x_ref.at[others], x_ref.at[others], zs).wait()
@@ -584,7 +586,7 @@
             pltpu.VMEM((2 * NCH, 4 * NCH), jnp.bfloat16),
             pltpu.VMEM((inputs, inputs), jnp.bfloat16),
             pltpu.VMEM((beams_n, inputs), jnp.int32),
-            pltpu.VMEM((2 * per * block, inputs), jnp.bfloat16),
+            pltpu.VMEM((2, 2 * per * block, inputs), jnp.bfloat16),
             pltpu.VMEM((n_grp, inputs, 2 * block), jnp.bfloat16),
             pltpu.VMEM((ch_dev, 2 * beams_n, inputs), jnp.bfloat16),
             pltpu.VMEM((per * n_chan * 128, 4 * per * beams_n), jnp.bfloat16),
@@ -792,7 +794,7 @@
     most = min(section, max(2, 2 * section // n_chan))
     fits = inp_dev == 64 and most == 32 and section == 64 and NCH == 128
     fits = fits and n_sub % 2 == 0 and ch_dev % (2 * QUAD) == 0 and inputs % 512 == 0
-    if not fits or n_sub != 4 or n_chan % 2 or n_chan > 8 or rows % 128:
+    if not fits or n_sub != 4 or n_chan & (n_chan - 1) or n_chan > 8 or rows % 128:
         return local_plain(voltages, taps, input_id, counts, delays, beam_owner)
     sub_index = lax.axis_index("sub")
     owner = beam_owner.reshape(1, -1)

time: 68.3 us -> 68 us (level)
  no operation moved by 1% of the time
where the time goes in v6:
time: 68 us; the launch traced here: 67.7 us
  Pallas kernels  66.8 us (98%)
  between operations  0.82 us (1%)
    pallas_call x1, Pallas kernels, front(): pl.pallas_call(functools.partial(front_kernel, n_chan, n_sub, most), in_s...  50.1 us
    pallas_call x1, Pallas kernels, back(): pl.pallas_call(back_kernel, in_specs=[smem, smem, hbm, hbm, pl.BlockSpec(...  16.8 us

profile of v6, /device:TPU:0, one launch (start us, length us, event | category | flops | bytes accessed | tf_op | source)
XLA Modules:
  0.0 67.7 jit_solution(11972119832336104739)
XLA Ops:
  0.6 50.1 %front.1 = (bf16[8,1024,256]{2,1,0:T(8,128)(2,1)}, bf16[4,4,2,64,128]{4,3,2,1,0:T(8,128)(2,1)}) custom-call(bf16[64,2,5504]{2,1,0:T(2,128)(2,1)} %volt_ref.1, f32[12,128]{1,0:T(8,128)} %bitcast.6, s32[4]{0:T(128)} %counts_ref.3, s32[1,1024]{1,0:T(1,128)} %bitcast.8, s32[64,1024]{1,0:T(8,128)} %delay_ref.1, s32[1,256]{1,0:T(1,128)} %bitcast.9), custom_call_target="tpu_custom_call" | custom-call | tf_op jit(solution)/shard_map/front/pallas_call | solution.py:565
  50.7 16.8 %back.1 = (bf16[32,2,256,1024]{3,2,1,0:T(8,128)(2,1)}, f32[32,2,5504]{2,1,0:T(2,128)}) custom-call(s32[1]{0:T(128)} %bitcast.sub_ref, s32[4]{0:T(128)} %counts_ref.3, bf16[8,1024,256]{2,1,0:T(8,128)(2,1)} %get-tuple-element.4.sorted_ref, bf16[4,8,64,128]{3,2,1,0:T(8,128)(2,1)} %bitcast.5, f32[12,128]{1,0:T(8,128)} %bitcast.7), custom_call_target="tpu_custom_call" | custom-call | tf_op jit(solution)/shard_map/back/pallas_call | solution.py:759
